TPU v7x, 256 devices: a whole 4x4x8 slice. The times are simulated.
256 devices in a mesh: dp: 16 (over x_lo, y, core), index: 16 (over z, x_hi).
Axes of the slice: x: 4 (x_hi: 2, x_lo: 2; x = x_hi * 2 + x_lo), y: 4, z: 8, core: 2. Of those that a mesh axis runs over, the one named last changes fastest.
Arguments:
- queries: bfloat16 [32768, 1024], P(('dp', 'index')), may hold values from -0.1875 to 0.1875
- keys: bfloat16 [16384, 1024], P(('dp', 'index')), may hold values from -6 to 6
- pattern: int32 [256, 256], P(('dp', 'index')), may hold values 0 or 1
- clusters: int32 [16384], P(('dp', 'index')), may hold values from 0 to 255
- positives: int32 [32768], P(('dp', 'index')), may hold values from 0 to 16383
- loss_multiplier: float32 [32768], P(('dp', 'index')), may hold values from -4 to 4
Outputs:
- query_grad: float32 [32768, 1024], P(('dp', 'index'))
- loss: float32 [32768], P(('dp', 'index'))
All inputs are finite; a program needn't handle non-finite values. No bound on the sum of `pattern` on one device may be relied on, other than what follows from the above.
Results may differ from a plain program's by a relative error of at most 0.0029.
Values may be sent and summed in bfloat16 or wider, within the bound.
A program may use at most 64 MiB of HBM per device.

v0:
```python
import jax
import jax.numpy as jnp
from jax import lax
from jax.sharding import PartitionSpec as P

logit_divisor = 0.1
epsilon = 1e-06


def shifted(value, axis, steps):
    count = lax.axis_size(axis)
    pairs = [(source, (source + steps) % count) for source in range(count)]
    return lax.ppermute(value, axis, pairs)


def unit_rows(values):
    floats = values.astype(jnp.float32)
    scaling = lax.rsqrt(jnp.sum(floats * floats, axis=1, keepdims=True) + epsilon)
    return (floats, scaling)


def tile_weights(key_tile, cluster_tile, first_key, gathered, pattern_rows, positive_indices):
    inner_product_matrix = (
        lax.dot_general(
            key_tile, gathered, (((1,), (1,)), ((), ())), preferred_element_type=jnp.float32
        )
        / logit_divisor
    )
    cluster_ids = cluster_tile.astype(jnp.int32)
    onehot = (
        cluster_ids[:, None] == jnp.arange(pattern_rows.shape[1], dtype=jnp.int32)[None, :]
    ).astype(jnp.float32)
    allowed = lax.dot_general(
        onehot, pattern_rows, (((1,), (1,)), ((), ())), precision=lax.Precision.HIGHEST
    )
    allowed = jnp.repeat(allowed, gathered.shape[0] // pattern_rows.shape[0], axis=1)
    key_ids = first_key + jnp.arange(key_tile.shape[0], dtype=jnp.int32)
    is_positive = (key_ids[:, None] == positive_indices[None, :]).astype(jnp.float32)
    weights = jnp.exp(inner_product_matrix) * jnp.maximum(allowed, is_positive)
    return (weights, jnp.sum(weights, axis=0), jnp.sum(inner_product_matrix * is_positive, axis=0))


def body(queries, keys, pattern, clusters, positives, loss_multiplier):
    query_floats, query_scale = unit_rows(queries)
    query_norm = (query_floats * query_scale).astype(jnp.bfloat16)
    key_floats, key_scale = unit_rows(keys)
    passage_magnitude = (key_floats * key_scale).astype(jnp.bfloat16)
    cluster_wire = clusters.astype(jnp.bfloat16)
    id_pair = jnp.stack([positives // 256, positives % 256], axis=1).astype(jnp.bfloat16)
    gathered, pattern_low, pair_rows = (
        lax.all_gather(query_norm, "dp", axis=0, tiled=True),
        lax.all_gather(pattern.astype(jnp.bfloat16), "dp", axis=0, tiled=True),
        lax.all_gather(id_pair, "dp", axis=0, tiled=True),
    )
    pattern_rows = pattern_low.astype(jnp.float32)
    pair_floats = pair_rows.astype(jnp.float32)
    positive_indices = (pair_floats[:, 0] * 256.0 + pair_floats[:, 1]).astype(jnp.int32)
    cycle_size = lax.axis_size("index")
    row_index = lax.axis_index("dp")
    col_index = lax.axis_index("index")
    tile_rows = keys.shape[0]
    total_rows = gathered.shape[0]
    row_base = row_index * cycle_size
    key_store = jnp.zeros((cycle_size, tile_rows, keys.shape[1]), jnp.bfloat16)
    weight_store = jnp.zeros((cycle_size, tile_rows, total_rows), jnp.bfloat16)
    carried = (
        key_store,
        weight_store,
        jnp.zeros((total_rows,), jnp.float32),
        jnp.zeros((total_rows,), jnp.float32),
    )

    def absorb(carried, slot_index, key_tile, cluster_tile, first_key, row_offset):
        key_store, weight_store, sums, positive_scores = carried
        weights, part_sums, part_scores = tile_weights(
            key_tile, cluster_tile, first_key, gathered, pattern_rows, positive_indices
        )
        offset_row = jnp.int32(row_offset)
        key_store = lax.dynamic_update_slice(
            key_store, key_tile[None], (slot_index, offset_row, jnp.int32(0))
        )
        weight_store = lax.dynamic_update_slice(
            weight_store, weights.astype(jnp.bfloat16)[None], (slot_index, offset_row, jnp.int32(0))
        )
        return (key_store, weight_store, sums + part_sums, positive_scores + part_scores)

    row_start = row_base * tile_rows
    offsets = positive_indices - row_start
    in_row = (offsets >= 0) & (offsets < cycle_size * tile_rows)
    safe_offsets = jnp.clip(offsets, 0, cycle_size * tile_rows - 1)
    source_ids = safe_offsets // tile_rows
    within = safe_offsets % tile_rows

    def cycle_turn(cycle_step, cycle_carry):
        carried, key_tile, cluster_tile = cycle_carry
        source = (col_index - cycle_step) % cycle_size
        carried = absorb(
            carried, cycle_step, key_tile, cluster_tile, (row_base + source) * tile_rows, 0
        )
        key_tile, cluster_tile = shifted((key_tile, cluster_tile), "index", 1)
        return (carried, key_tile, cluster_tile)

    carried, key_tile, cluster_tile = lax.fori_loop(
        0, cycle_size - 1, cycle_turn, (carried, passage_magnitude, cluster_wire)
    )
    last_step = jnp.int32(cycle_size - 1)
    source = (col_index - last_step) % cycle_size
    carried = absorb(carried, last_step, key_tile, cluster_tile, (row_base + source) * tile_rows, 0)
    slots = (col_index - source_ids) % cycle_size
    key_store, weight_store, sums, positive_scores = carried
    expected = lax.dot_general(
        weight_store, key_store, (((0, 1), (0, 1)), ((), ())), preferred_element_type=jnp.float32
    )
    flat_keys = key_store.reshape(cycle_size * tile_rows, key_store.shape[2])
    picked = flat_keys[slots * tile_rows + within]
    selected_lower = jnp.where(in_row[:, None], picked, jnp.zeros_like(picked))
    mine_expected, mine_positive, mine_sums, mine_scores = (
        lax.psum_scatter(expected, "dp", scatter_dimension=0, tiled=True),
        lax.psum_scatter(selected_lower.astype(jnp.float32), "dp", scatter_dimension=0, tiled=True),
        lax.psum_scatter(sums, "dp", scatter_dimension=0, tiled=True),
        lax.psum_scatter(positive_scores, "dp", scatter_dimension=0, tiled=True),
    )
    update_direction_entry = mine_expected / mine_sums[:, None] - mine_positive
    question_derivative = update_direction_entry * (loss_multiplier / logit_divisor)[:, None]
    projection = jnp.sum(query_floats * question_derivative, axis=1, keepdims=True)
    query_grad = (
        query_scale * question_derivative
        - query_scale * query_scale * query_scale * query_floats * projection
    )
    loss_values = jnp.log(mine_sums) - mine_scores
    return (query_grad, loss_values)


def solution(mesh):
    in_specs = (
        P(("dp", "index"), None),
        P(("dp", "index"), None),
        P(("dp", "index"), None),
        P(("dp", "index")),
        P(("dp", "index")),
        P(("dp", "index")),
    )
    out_specs = (P(("dp", "index"), None), P(("dp", "index")))
    return jax.shard_map(body, mesh=mesh, in_specs=in_specs, out_specs=out_specs, check_vma=False)
```

profile of v0, /device:TPU:1, one launch (start us, length us, event | category | flops | bytes accessed | tf_op | source)
XLA Modules:
  0.0 374.8 jit_solution(12083205661405783855)
XLA Ops:
  10.9 21.1 %all_gather.11 = bf16[2048,2]{0,1:T(2,128)(2,1)S(1)} all-gather(bf16[128,2]{0,1:T(2,128)(2,1)S(1)} %pad_maximum_fusion), channel_id=1, replica_groups=mesh['dp'=16,'index'=16] {'dp'}, dimensions={0}, use_global_device_ids=true | all-gather | bytes 8704 | tf_op jit(solution)/shard_map/all_gather | solution.py:53
  33.3 16.2 %all-gather = bf16[16,1,256]{2,1,0:T(2,128)(2,1)S(1)} all-gather(bf16[1,1,256]{2,1,0:T(2,128)(2,1)S(1)} %convert_bitcast_fusion), channel_id=1, replica_groups=mesh['dp'=16,'index'=16] {'dp'}, dimensions={0}, use_global_device_ids=true | all-gather | bytes 8704 | tf_op jit(solution)/shard_map/all_gather | solution.py:52
  57.5 135.5 %while.26 = (s32[]{:T(128)}, bf16[16,64,1024]{2,1,0:T(8,128)(2,1)S(1)}, bf16[16,64,2048]{2,1,0:T(8,128)(2,1)}, f32[2048]{0:T(1024)S(1)}, f32[2048]{0:T(1024)S(1)...) while((s32[]{:T(128)}, ...), condition=%wide.region_5.6_spmd.clone, body=%wide.region_2.5_spmd.clone.sunk | while | flops 273305728 | bytes 8367120 | solution.py:103
  62.1 4.4 %bitcast_dynamic-update-slice_fusion.7 = (bf16[16,64,2048]{2,1,0:T(8,128)(2,1)}, f32[64,2048]{1,0:T(8,128)S(1)}) fusion(bf16[16,64,2048]{2,1,0:T(8,128)(2,1)} %get-tuple-element.487, s32[]{:T(128)} %get-tuple-element.485, s32[2048]{0:T(1024)S(1)} %get-tuple-element.513, s32[64]{0:T(128)S(1)} %iota_add_fusion.3, f32[8,8,16,128]{3,2,1,0:T(8,128)S(1)} %bitcast.60, ...), kind=kOutput, calls=%fused_computation.7.clone.1 | convolution fusion | flops 269221888 | bytes 5645056 | tf_op jit(solution)/shard_map/while/body/eval_jaxpr/dot_general | solution.py:24
  71.3 4.4 %bitcast_dynamic-update-slice_fusion.7 = (bf16[16,64,2048]{2,1,0:T(8,128)(2,1)}, f32[64,2048]{1,0:T(8,128)S(1)}) fusion(bf16[16,64,2048]{2,1,0:T(8,128)(2,1)} %get-tuple-element.487, s32[]{:T(128)} %get-tuple-element.485, s32[2048]{0:T(1024)S(1)} %get-tuple-element.513, s32[64]{0:T(128)S(1)} %iota_add_fusion.3, f32[8,8,16,128]{3,2,1,0:T(8,128)S(1)} %bitcast.60, ...), kind=kOutput, calls=%fused_computation.7.clone.1 | convolution fusion | flops 269221888 | bytes 5645056 | tf_op jit(solution)/shard_map/while/body/eval_jaxpr/dot_general | solution.py:24
  80.6 4.4 %bitcast_dynamic-update-slice_fusion.7 = (bf16[16,64,2048]{2,1,0:T(8,128)(2,1)}, f32[64,2048]{1,0:T(8,128)S(1)}) fusion(bf16[16,64,2048]{2,1,0:T(8,128)(2,1)} %get-tuple-element.487, s32[]{:T(128)} %get-tuple-element.485, s32[2048]{0:T(1024)S(1)} %get-tuple-element.513, s32[64]{0:T(128)S(1)} %iota_add_fusion.3, f32[8,8,16,128]{3,2,1,0:T(8,128)S(1)} %bitcast.60, ...), kind=kOutput, calls=%fused_computation.7.clone.1 | convolution fusion | flops 269221888 | bytes 5645056 | tf_op jit(solution)/shard_map/while/body/eval_jaxpr/dot_general | solution.py:24
  91.0 4.4 %bitcast_dynamic-update-slice_fusion.7 = (bf16[16,64,2048]{2,1,0:T(8,128)(2,1)}, f32[64,2048]{1,0:T(8,128)S(1)}) fusion(bf16[16,64,2048]{2,1,0:T(8,128)(2,1)} %get-tuple-element.487, s32[]{:T(128)} %get-tuple-element.485, s32[2048]{0:T(1024)S(1)} %get-tuple-element.513, s32[64]{0:T(128)S(1)} %iota_add_fusion.3, f32[8,8,16,128]{3,2,1,0:T(8,128)S(1)} %bitcast.60, ...), kind=kOutput, calls=%fused_computation.7.clone.1 | convolution fusion | flops 269221888 | bytes 5645056 | tf_op jit(solution)/shard_map/while/body/eval_jaxpr/dot_general | solution.py:24
  99.9 4.4 %bitcast_dynamic-update-slice_fusion.7 = (bf16[16,64,2048]{2,1,0:T(8,128)(2,1)}, f32[64,2048]{1,0:T(8,128)S(1)}) fusion(bf16[16,64,2048]{2,1,0:T(8,128)(2,1)} %get-tuple-element.487, s32[]{:T(128)} %get-tuple-element.485, s32[2048]{0:T(1024)S(1)} %get-tuple-element.513, s32[64]{0:T(128)S(1)} %iota_add_fusion.3, f32[8,8,16,128]{3,2,1,0:T(8,128)S(1)} %bitcast.60, ...), kind=kOutput, calls=%fused_computation.7.clone.1 | convolution fusion | flops 269221888 | bytes 5645056 | tf_op jit(solution)/shard_map/while/body/eval_jaxpr/dot_general | solution.py:24
  108.1 4.4 %bitcast_dynamic-update-slice_fusion.7 = (bf16[16,64,2048]{2,1,0:T(8,128)(2,1)}, f32[64,2048]{1,0:T(8,128)S(1)}) fusion(bf16[16,64,2048]{2,1,0:T(8,128)(2,1)} %get-tuple-element.487, s32[]{:T(128)} %get-tuple-element.485, s32[2048]{0:T(1024)S(1)} %get-tuple-element.513, s32[64]{0:T(128)S(1)} %iota_add_fusion.3, f32[8,8,16,128]{3,2,1,0:T(8,128)S(1)} %bitcast.60, ...), kind=kOutput, calls=%fused_computation.7.clone.1 | convolution fusion | flops 269221888 | bytes 5645056 | tf_op jit(solution)/shard_map/while/body/eval_jaxpr/dot_general | solution.py:24
  116.3 4.4 %bitcast_dynamic-update-slice_fusion.7 = (bf16[16,64,2048]{2,1,0:T(8,128)(2,1)}, f32[64,2048]{1,0:T(8,128)S(1)}) fusion(bf16[16,64,2048]{2,1,0:T(8,128)(2,1)} %get-tuple-element.487, s32[]{:T(128)} %get-tuple-element.485, s32[2048]{0:T(1024)S(1)} %get-tuple-element.513, s32[64]{0:T(128)S(1)} %iota_add_fusion.3, f32[8,8,16,128]{3,2,1,0:T(8,128)S(1)} %bitcast.60, ...), kind=kOutput, calls=%fused_computation.7.clone.1 | convolution fusion | flops 269221888 | bytes 5645056 | tf_op jit(solution)/shard_map/while/body/eval_jaxpr/dot_general | solution.py:24
  124.6 4.4 %bitcast_dynamic-update-slice_fusion.7 = (bf16[16,64,2048]{2,1,0:T(8,128)(2,1)}, f32[64,2048]{1,0:T(8,128)S(1)}) fusion(bf16[16,64,2048]{2,1,0:T(8,128)(2,1)} %get-tuple-element.487, s32[]{:T(128)} %get-tuple-element.485, s32[2048]{0:T(1024)S(1)} %get-tuple-element.513, s32[64]{0:T(128)S(1)} %iota_add_fusion.3, f32[8,8,16,128]{3,2,1,0:T(8,128)S(1)} %bitcast.60, ...), kind=kOutput, calls=%fused_computation.7.clone.1 | convolution fusion | flops 269221888 | bytes 5645056 | tf_op jit(solution)/shard_map/while/body/eval_jaxpr/dot_general | solution.py:24
  133.3 4.4 %bitcast_dynamic-update-slice_fusion.7 = (bf16[16,64,2048]{2,1,0:T(8,128)(2,1)}, f32[64,2048]{1,0:T(8,128)S(1)}) fusion(bf16[16,64,2048]{2,1,0:T(8,128)(2,1)} %get-tuple-element.487, s32[]{:T(128)} %get-tuple-element.485, s32[2048]{0:T(1024)S(1)} %get-tuple-element.513, s32[64]{0:T(128)S(1)} %iota_add_fusion.3, f32[8,8,16,128]{3,2,1,0:T(8,128)S(1)} %bitcast.60, ...), kind=kOutput, calls=%fused_computation.7.clone.1 | convolution fusion | flops 269221888 | bytes 5645056 | tf_op jit(solution)/shard_map/while/body/eval_jaxpr/dot_general | solution.py:24
  142.6 4.4 %bitcast_dynamic-update-slice_fusion.7 = (bf16[16,64,2048]{2,1,0:T(8,128)(2,1)}, f32[64,2048]{1,0:T(8,128)S(1)}) fusion(bf16[16,64,2048]{2,1,0:T(8,128)(2,1)} %get-tuple-element.487, s32[]{:T(128)} %get-tuple-element.485, s32[2048]{0:T(1024)S(1)} %get-tuple-element.513, s32[64]{0:T(128)S(1)} %iota_add_fusion.3, f32[8,8,16,128]{3,2,1,0:T(8,128)S(1)} %bitcast.60, ...), kind=kOutput, calls=%fused_computation.7.clone.1 | convolution fusion | flops 269221888 | bytes 5645056 | tf_op jit(solution)/shard_map/while/body/eval_jaxpr/dot_general | solution.py:24
  151.9 4.4 %bitcast_dynamic-update-slice_fusion.7 = (bf16[16,64,2048]{2,1,0:T(8,128)(2,1)}, f32[64,2048]{1,0:T(8,128)S(1)}) fusion(bf16[16,64,2048]{2,1,0:T(8,128)(2,1)} %get-tuple-element.487, s32[]{:T(128)} %get-tuple-element.485, s32[2048]{0:T(1024)S(1)} %get-tuple-element.513, s32[64]{0:T(128)S(1)} %iota_add_fusion.3, f32[8,8,16,128]{3,2,1,0:T(8,128)S(1)} %bitcast.60, ...), kind=kOutput, calls=%fused_computation.7.clone.1 | convolution fusion | flops 269221888 | bytes 5645056 | tf_op jit(solution)/shard_map/while/body/eval_jaxpr/dot_general | solution.py:24
  162.2 4.4 %bitcast_dynamic-update-slice_fusion.7 = (bf16[16,64,2048]{2,1,0:T(8,128)(2,1)}, f32[64,2048]{1,0:T(8,128)S(1)}) fusion(bf16[16,64,2048]{2,1,0:T(8,128)(2,1)} %get-tuple-element.487, s32[]{:T(128)} %get-tuple-element.485, s32[2048]{0:T(1024)S(1)} %get-tuple-element.513, s32[64]{0:T(128)S(1)} %iota_add_fusion.3, f32[8,8,16,128]{3,2,1,0:T(8,128)S(1)} %bitcast.60, ...), kind=kOutput, calls=%fused_computation.7.clone.1 | convolution fusion | flops 269221888 | bytes 5645056 | tf_op jit(solution)/shard_map/while/body/eval_jaxpr/dot_general | solution.py:24
  171.1 4.4 %bitcast_dynamic-update-slice_fusion.7 = (bf16[16,64,2048]{2,1,0:T(8,128)(2,1)}, f32[64,2048]{1,0:T(8,128)S(1)}) fusion(bf16[16,64,2048]{2,1,0:T(8,128)(2,1)} %get-tuple-element.487, s32[]{:T(128)} %get-tuple-element.485, s32[2048]{0:T(1024)S(1)} %get-tuple-element.513, s32[64]{0:T(128)S(1)} %iota_add_fusion.3, f32[8,8,16,128]{3,2,1,0:T(8,128)S(1)} %bitcast.60, ...), kind=kOutput, calls=%fused_computation.7.clone.1 | convolution fusion | flops 269221888 | bytes 5645056 | tf_op jit(solution)/shard_map/while/body/eval_jaxpr/dot_general | solution.py:24
  179.3 4.4 %bitcast_dynamic-update-slice_fusion.7 = (bf16[16,64,2048]{2,1,0:T(8,128)(2,1)}, f32[64,2048]{1,0:T(8,128)S(1)}) fusion(bf16[16,64,2048]{2,1,0:T(8,128)(2,1)} %get-tuple-element.487, s32[]{:T(128)} %get-tuple-element.485, s32[2048]{0:T(1024)S(1)} %get-tuple-element.513, s32[64]{0:T(128)S(1)} %iota_add_fusion.3, f32[8,8,16,128]{3,2,1,0:T(8,128)S(1)} %bitcast.60, ...), kind=kOutput, calls=%fused_computation.7.clone.1 | convolution fusion | flops 269221888 | bytes 5645056 | tf_op jit(solution)/shard_map/while/body/eval_jaxpr/dot_general | solution.py:24
  187.5 4.4 %bitcast_dynamic-update-slice_fusion.7 = (bf16[16,64,2048]{2,1,0:T(8,128)(2,1)}, f32[64,2048]{1,0:T(8,128)S(1)}) fusion(bf16[16,64,2048]{2,1,0:T(8,128)(2,1)} %get-tuple-element.487, s32[]{:T(128)} %get-tuple-element.485, s32[2048]{0:T(1024)S(1)} %get-tuple-element.513, s32[64]{0:T(128)S(1)} %iota_add_fusion.3, f32[8,8,16,128]{3,2,1,0:T(8,128)S(1)} %bitcast.60, ...), kind=kOutput, calls=%fused_computation.7.clone.1 | convolution fusion | flops 269221888 | bytes 5645056 | tf_op jit(solution)/shard_map/while/body/eval_jaxpr/dot_general | solution.py:24
  193.5 4.4 %bitcast_dynamic-update-slice_fusion.2 = (bf16[16,64,2048]{2,1,0:T(8,128)(2,1)}, f32[64,2048]{1,0:T(8,128)S(1)}) fusion(bf16[16,64,2048]{2,1,0:T(8,128)(2,1)} %get-tuple-element.294, s32[2048]{0:T(1024)S(1)} %get-tuple-element.532, s32[64]{0:T(128)S(1)} %iota_add_fusion.1, f32[8,8,16,128]{3,2,1,0:T(8,128)S(1)} %bitcast.62, ...), kind=kOutput, calls=%fused_computation.38 | convolution fusion | flops 269221888 | bytes 5644544 | tf_op jit(solution)/shard_map/dot_general | solution.py:24
  197.8 9.0 %convolution_bitcast_fusion = f32[2048,1024]{1,0:T(8,128)} fusion(bf16[16,64,2048]{2,1,0:T(8,128)(2,1)} %get-tuple-element.381, bf16[16,64,1024]{2,1,0:T(8,128)(2,1)S(1)} %bitcast_dynamic-update-slice_fusion.3), kind=kOutput, calls=%fused_computation.16 | convolution fusion | flops 4294967296 | bytes 14680064 | tf_op jit(solution)/shard_map/dot_general | solution.py:111
  207.1 9.7 %gather_fusion = bf16[2048,1024]{1,0:T(8,128)(2,1)} fusion(bf16[1024,1024]{1,0:T(8,128)(2,1)S(1)} %bitcast.59, s32[2048]{0:T(1024)S(1)} %broadcast_clamp_fusion), kind=kCustom, calls=%fused_computation | custom fusion | bytes 8396800 | tf_op jit(solution)/shard_map/gather | solution.py:115
  216.8 5.1 %select_convert_fusion = f32[2048,1024]{1,0:T(8,128)} fusion(bf16[2048,1024]{1,0:T(8,128)(2,1)} %gather_fusion, pred[2048]{0:T(1024)(128)(4,1)S(1)} %get-tuple-element.369), kind=kLoop, calls=%fused_computation.17 | loop fusion | flops 4194304 | bytes 12584960 | tf_op jit(solution)/shard_map/convert_element_type | solution.py:119
  224.2 58.4 %all-reduce.2 = (f32[2048]{0:T(1024)S(1)}, f32[2048]{0:T(1024)S(1)}) all-reduce(f32[2048]{0:T(1024)S(1)} %add.194, f32[2048]{0:T(1024)S(1)} %add.199), channel_id=3, replica_groups=mesh['dp'=16,'index'=16] {'dp'}, use_global_device_ids=true, to_apply=%region_8.9.clone | all-reduce | flops 4096 | bytes 32768
  286.2 78.3 %reduce-scatter.5.cloned.1.call-done = f32[128,1024]{1,0:T(8,128)} async-done(((f32[2048,1024]{1,0:T(8,128)}), f32[128,1024]{1,0:T(8,128)}) %reduce-scatter.5.cloned.1.call-update) | async-done | bytes 524304 | tf_op jit(solution)/shard_map/reduce_scatter | solution.py:119
  (241 shorter events, 91.0 us)
Async XLA Ops:
  7.2 47.6 %all-gather.3.cloned.1.call-start = ((), (), s32[]{:S(2)}) async-start(), calls=%async_computation.2 | async-start | bytes 4456448 | tf_op jit(solution)/shard_map/all_gather | solution.py:51
  10.1 276.1 %reduce-scatter.3.cloned.1.call-start = ((), (), s32[]{:S(2)}) async-start(), calls=%async_computation.3 | async-start | bytes 8912896 | tf_op jit(solution)/shard_map/reduce_scatter | solution.py:118
  57.6 9.3 %collective-permute-start = (bf16[64,1024]{1,0:T(8,128)(2,1)S(1)}, bf16[64,1024]{1,0:T(8,128)(2,1)S(1)}, u32[]{:S(2)}, u32[]{:S(2)}) collective-permute-start(bf16[64,1024]{1,0:T(8,128)(2,1)S(1)} %copy.50), channel_id=1, source_target_pairs={{0,1},{1,2},{2,3},{3,4},{4,5},{5,6},{6,7},{7,8},{8,9},{9,10},{10,1... | collective-permute-start | bytes 393224 | tf_op jit(solution)/shard_map/while/body/eval_jaxpr/ppermute | solution.py:13
  66.9 9.2 %collective-permute-start = (bf16[64,1024]{1,0:T(8,128)(2,1)S(1)}, bf16[64,1024]{1,0:T(8,128)(2,1)S(1)}, u32[]{:S(2)}, u32[]{:S(2)}) collective-permute-start(bf16[64,1024]{1,0:T(8,128)(2,1)S(1)} %copy.50), channel_id=1, source_target_pairs={{0,1},{1,2},{2,3},{3,4},{4,5},{5,6},{6,7},{7,8},{8,9},{9,10},{10,1... | collective-permute-start | bytes 393224 | tf_op jit(solution)/shard_map/while/body/eval_jaxpr/ppermute | solution.py:13
  76.1 9.3 %collective-permute-start = (bf16[64,1024]{1,0:T(8,128)(2,1)S(1)}, bf16[64,1024]{1,0:T(8,128)(2,1)S(1)}, u32[]{:S(2)}, u32[]{:S(2)}) collective-permute-start(bf16[64,1024]{1,0:T(8,128)(2,1)S(1)} %copy.50), channel_id=1, source_target_pairs={{0,1},{1,2},{2,3},{3,4},{4,5},{5,6},{6,7},{7,8},{8,9},{9,10},{10,1... | collective-permute-start | bytes 393224 | tf_op jit(solution)/shard_map/while/body/eval_jaxpr/ppermute | solution.py:13
  78.6 6.8 %collective-permute-start.1 = (bf16[64]{0:T(256)(128)(2,1)S(1)}, bf16[64]{0:T(256)(128)(2,1)S(1)}, u32[]{:S(2)}, u32[]{:S(2)}) collective-permute-start(bf16[64]{0:T(256)(128)(2,1)S(1)} %copy.51), channel_id=1, source_target_pairs={{0,1},{1,2},{2,3},{3,4},{4,5},{5,6},{6,7},{7,8},{8,9},{9,10},{10,1... | collective-permute-start | bytes 392 | tf_op jit(solution)/shard_map/while/body/eval_jaxpr/ppermute | solution.py:13
  85.5 10.3 %collective-permute-start = (bf16[64,1024]{1,0:T(8,128)(2,1)S(1)}, bf16[64,1024]{1,0:T(8,128)(2,1)S(1)}, u32[]{:S(2)}, u32[]{:S(2)}) collective-permute-start(bf16[64,1024]{1,0:T(8,128)(2,1)S(1)} %copy.50), channel_id=1, source_target_pairs={{0,1},{1,2},{2,3},{3,4},{4,5},{5,6},{6,7},{7,8},{8,9},{9,10},{10,1... | collective-permute-start | bytes 393224 | tf_op jit(solution)/shard_map/while/body/eval_jaxpr/ppermute | solution.py:13
  87.8 8.0 %collective-permute-start.1 = (bf16[64]{0:T(256)(128)(2,1)S(1)}, bf16[64]{0:T(256)(128)(2,1)S(1)}, u32[]{:S(2)}, u32[]{:S(2)}) collective-permute-start(bf16[64]{0:T(256)(128)(2,1)S(1)} %copy.51), channel_id=1, source_target_pairs={{0,1},{1,2},{2,3},{3,4},{4,5},{5,6},{6,7},{7,8},{8,9},{9,10},{10,1... | collective-permute-start | bytes 392 | tf_op jit(solution)/shard_map/while/body/eval_jaxpr/ppermute | solution.py:13
  95.8 8.8 %collective-permute-start = (bf16[64,1024]{1,0:T(8,128)(2,1)S(1)}, bf16[64,1024]{1,0:T(8,128)(2,1)S(1)}, u32[]{:S(2)}, u32[]{:S(2)}) collective-permute-start(bf16[64,1024]{1,0:T(8,128)(2,1)S(1)} %copy.50), channel_id=1, source_target_pairs={{0,1},{1,2},{2,3},{3,4},{4,5},{5,6},{6,7},{7,8},{8,9},{9,10},{10,1... | collective-permute-start | bytes 393224 | tf_op jit(solution)/shard_map/while/body/eval_jaxpr/ppermute | solution.py:13
  104.7 8.3 %collective-permute-start = (bf16[64,1024]{1,0:T(8,128)(2,1)S(1)}, bf16[64,1024]{1,0:T(8,128)(2,1)S(1)}, u32[]{:S(2)}, u32[]{:S(2)}) collective-permute-start(bf16[64,1024]{1,0:T(8,128)(2,1)S(1)} %copy.50), channel_id=1, source_target_pairs={{0,1},{1,2},{2,3},{3,4},{4,5},{5,6},{6,7},{7,8},{8,9},{9,10},{10,1... | collective-permute-start | bytes 393224 | tf_op jit(solution)/shard_map/while/body/eval_jaxpr/ppermute | solution.py:13
  113.0 8.1 %collective-permute-start = (bf16[64,1024]{1,0:T(8,128)(2,1)S(1)}, bf16[64,1024]{1,0:T(8,128)(2,1)S(1)}, u32[]{:S(2)}, u32[]{:S(2)}) collective-permute-start(bf16[64,1024]{1,0:T(8,128)(2,1)S(1)} %copy.50), channel_id=1, source_target_pairs={{0,1},{1,2},{2,3},{3,4},{4,5},{5,6},{6,7},{7,8},{8,9},{9,10},{10,1... | collective-permute-start | bytes 393224 | tf_op jit(solution)/shard_map/while/body/eval_jaxpr/ppermute | solution.py:13
  121.1 8.4 %collective-permute-start = (bf16[64,1024]{1,0:T(8,128)(2,1)S(1)}, bf16[64,1024]{1,0:T(8,128)(2,1)S(1)}, u32[]{:S(2)}, u32[]{:S(2)}) collective-permute-start(bf16[64,1024]{1,0:T(8,128)(2,1)S(1)} %copy.50), channel_id=1, source_target_pairs={{0,1},{1,2},{2,3},{3,4},{4,5},{5,6},{6,7},{7,8},{8,9},{9,10},{10,1... | collective-permute-start | bytes 393224 | tf_op jit(solution)/shard_map/while/body/eval_jaxpr/ppermute | solution.py:13
  129.5 8.6 %collective-permute-start = (bf16[64,1024]{1,0:T(8,128)(2,1)S(1)}, bf16[64,1024]{1,0:T(8,128)(2,1)S(1)}, u32[]{:S(2)}, u32[]{:S(2)}) collective-permute-start(bf16[64,1024]{1,0:T(8,128)(2,1)S(1)} %copy.50), channel_id=1, source_target_pairs={{0,1},{1,2},{2,3},{3,4},{4,5},{5,6},{6,7},{7,8},{8,9},{9,10},{10,1... | collective-permute-start | bytes 393224 | tf_op jit(solution)/shard_map/while/body/eval_jaxpr/ppermute | solution.py:13
  131.3 6.8 %collective-permute-start.1 = (bf16[64]{0:T(256)(128)(2,1)S(1)}, bf16[64]{0:T(256)(128)(2,1)S(1)}, u32[]{:S(2)}, u32[]{:S(2)}) collective-permute-start(bf16[64]{0:T(256)(128)(2,1)S(1)} %copy.51), channel_id=1, source_target_pairs={{0,1},{1,2},{2,3},{3,4},{4,5},{5,6},{6,7},{7,8},{8,9},{9,10},{10,1... | collective-permute-start | bytes 392 | tf_op jit(solution)/shard_map/while/body/eval_jaxpr/ppermute | solution.py:13
  138.1 9.2 %collective-permute-start = (bf16[64,1024]{1,0:T(8,128)(2,1)S(1)}, bf16[64,1024]{1,0:T(8,128)(2,1)S(1)}, u32[]{:S(2)}, u32[]{:S(2)}) collective-permute-start(bf16[64,1024]{1,0:T(8,128)(2,1)S(1)} %copy.50), channel_id=1, source_target_pairs={{0,1},{1,2},{2,3},{3,4},{4,5},{5,6},{6,7},{7,8},{8,9},{9,10},{10,1... | collective-permute-start | bytes 393224 | tf_op jit(solution)/shard_map/while/body/eval_jaxpr/ppermute | solution.py:13
  147.4 9.3 %collective-permute-start = (bf16[64,1024]{1,0:T(8,128)(2,1)S(1)}, bf16[64,1024]{1,0:T(8,128)(2,1)S(1)}, u32[]{:S(2)}, u32[]{:S(2)}) collective-permute-start(bf16[64,1024]{1,0:T(8,128)(2,1)S(1)} %copy.50), channel_id=1, source_target_pairs={{0,1},{1,2},{2,3},{3,4},{4,5},{5,6},{6,7},{7,8},{8,9},{9,10},{10,1... | collective-permute-start | bytes 393224 | tf_op jit(solution)/shard_map/while/body/eval_jaxpr/ppermute | solution.py:13
  149.9 6.8 %collective-permute-start.1 = (bf16[64]{0:T(256)(128)(2,1)S(1)}, bf16[64]{0:T(256)(128)(2,1)S(1)}, u32[]{:S(2)}, u32[]{:S(2)}) collective-permute-start(bf16[64]{0:T(256)(128)(2,1)S(1)} %copy.51), channel_id=1, source_target_pairs={{0,1},{1,2},{2,3},{3,4},{4,5},{5,6},{6,7},{7,8},{8,9},{9,10},{10,1... | collective-permute-start | bytes 392 | tf_op jit(solution)/shard_map/while/body/eval_jaxpr/ppermute | solution.py:13
  156.7 10.3 %collective-permute-start = (bf16[64,1024]{1,0:T(8,128)(2,1)S(1)}, bf16[64,1024]{1,0:T(8,128)(2,1)S(1)}, u32[]{:S(2)}, u32[]{:S(2)}) collective-permute-start(bf16[64,1024]{1,0:T(8,128)(2,1)S(1)} %copy.50), channel_id=1, source_target_pairs={{0,1},{1,2},{2,3},{3,4},{4,5},{5,6},{6,7},{7,8},{8,9},{9,10},{10,1... | collective-permute-start | bytes 393224 | tf_op jit(solution)/shard_map/while/body/eval_jaxpr/ppermute | solution.py:13
  159.0 8.0 %collective-permute-start.1 = (bf16[64]{0:T(256)(128)(2,1)S(1)}, bf16[64]{0:T(256)(128)(2,1)S(1)}, u32[]{:S(2)}, u32[]{:S(2)}) collective-permute-start(bf16[64]{0:T(256)(128)(2,1)S(1)} %copy.51), channel_id=1, source_target_pairs={{0,1},{1,2},{2,3},{3,4},{4,5},{5,6},{6,7},{7,8},{8,9},{9,10},{10,1... | collective-permute-start | bytes 392 | tf_op jit(solution)/shard_map/while/body/eval_jaxpr/ppermute | solution.py:13
  167.0 8.8 %collective-permute-start = (bf16[64,1024]{1,0:T(8,128)(2,1)S(1)}, bf16[64,1024]{1,0:T(8,128)(2,1)S(1)}, u32[]{:S(2)}, u32[]{:S(2)}) collective-permute-start(bf16[64,1024]{1,0:T(8,128)(2,1)S(1)} %copy.50), channel_id=1, source_target_pairs={{0,1},{1,2},{2,3},{3,4},{4,5},{5,6},{6,7},{7,8},{8,9},{9,10},{10,1... | collective-permute-start | bytes 393224 | tf_op jit(solution)/shard_map/while/body/eval_jaxpr/ppermute | solution.py:13
  175.9 8.2 %collective-permute-start = (bf16[64,1024]{1,0:T(8,128)(2,1)S(1)}, bf16[64,1024]{1,0:T(8,128)(2,1)S(1)}, u32[]{:S(2)}, u32[]{:S(2)}) collective-permute-start(bf16[64,1024]{1,0:T(8,128)(2,1)S(1)} %copy.50), channel_id=1, source_target_pairs={{0,1},{1,2},{2,3},{3,4},{4,5},{5,6},{6,7},{7,8},{8,9},{9,10},{10,1... | collective-permute-start | bytes 393224 | tf_op jit(solution)/shard_map/while/body/eval_jaxpr/ppermute | solution.py:13
  184.1 8.9 %collective-permute-start = (bf16[64,1024]{1,0:T(8,128)(2,1)S(1)}, bf16[64,1024]{1,0:T(8,128)(2,1)S(1)}, u32[]{:S(2)}, u32[]{:S(2)}) collective-permute-start(bf16[64,1024]{1,0:T(8,128)(2,1)S(1)} %copy.50), channel_id=1, source_target_pairs={{0,1},{1,2},{2,3},{3,4},{4,5},{5,6},{6,7},{7,8},{8,9},{9,10},{10,1... | collective-permute-start | bytes 393224 | tf_op jit(solution)/shard_map/while/body/eval_jaxpr/ppermute | solution.py:13
  186.3 6.8 %collective-permute-start.1 = (bf16[64]{0:T(256)(128)(2,1)S(1)}, bf16[64]{0:T(256)(128)(2,1)S(1)}, u32[]{:S(2)}, u32[]{:S(2)}) collective-permute-start(bf16[64]{0:T(256)(128)(2,1)S(1)} %copy.51), channel_id=1, source_target_pairs={{0,1},{1,2},{2,3},{3,4},{4,5},{5,6},{6,7},{7,8},{8,9},{9,10},{10,1... | collective-permute-start | bytes 392 | tf_op jit(solution)/shard_map/while/body/eval_jaxpr/ppermute | solution.py:13
  206.9 157.6 %reduce-scatter.5.cloned.1.call-start = ((), (), s32[]{:S(2)}) async-start(), calls=%async_computation.4 | async-start | bytes 8912896 | tf_op jit(solution)/shard_map/reduce_scatter | solution.py:119
  (12 other events, 202.7 us)
Sparse Core Ops, SparseCore 0:
  10.4 44.3 all-gather.2
  207.0 79.1 reduce-scatter.2
  288.8 75.7 reduce-scatter.4
where the time goes:
time: 378 us; the launch traced here: 375 us
  blocking collectives  95.7 us (25%)
  waiting for transfers between devices  85.5 us (23%)
  matrix products  82.8 us (22%)
  starting transfers between devices  56 us (15%)
  other arithmetic  22.1 us (6%)
  local copies, waits for them, and re-layouts  17.1 us (5%)
  between operations  14.6 us (4%)
    reduce_scatter x1, waiting for transfers between devices, body(): lax.psum_scatter(selected_lower.astype(jnp.float32), 'dp', scatter_dimens...  78.3 us
    dot_general x16, matrix products, tile_weights(): lax.dot_general(key_tile, gathered, (((1,), (1,)), ((), ())), preferred_e...  70.2 us
    unnamed x1, blocking collectives  58.4 us
    ppermute x30, starting transfers between devices, shifted(): return lax.ppermute(value, axis, pairs)  55.9 us
    all_gather x1, blocking collectives, body(): lax.all_gather(id_pair, 'dp', axis=0, tiled=True)  21.1 us
    all_gather x1, blocking collectives, body(): lax.all_gather(pattern.astype(jnp.bfloat16), 'dp', axis=0, tiled=True)  16.2 us
    gather x1, local copies, waits for them, and re-layouts, body(): picked = flat_keys[slots * tile_rows + within]  9.68 us
    dot_general x1, matrix products, body(): lax.dot_general(weight_store, key_store, (((0, 1), (0, 1)), ((), ())), pr...  9.05 us
  transfers between devices with their start and end apart: 33, of which 4 were waited for; matrix products, arithmetic and copies ran while one was open for 26% of the time, Pallas kernels for 0%

commit v1 on v0

v1 whole, which is shorter than its diff:
```python
import functools
import math

import jax
import jax.numpy as jnp
from jax import lax
from jax.experimental import pallas as pl
from jax.experimental.pallas import tpu as pltpu
from jax.sharding import PartitionSpec as P

MESH = pl.DeviceIdType.MESH
EPS = 1e-06
NX, NY, NZ = 4, 4, 8
EXP2_SCALE = 10.0 * math.log2(math.e)
F32, BF16, I32 = jnp.float32, jnp.bfloat16, jnp.int32


def unit_of(k):
    if k == 0:
        return 0
    if k == 4:
        return 14
    return 2 + 4 * (k - 1) if k < 4 else 2 + 4 * (7 - k) + 1


def sibling_unit(k):
    return unit_of(k) + (1 if k in (0, 4) else 2)


class Ids:
    def __init__(self):
        self.names = {}

    def __call__(self, *name):
        return self.names.setdefault(name, len(self.names))


def message_names():
    ids = Ids()
    for d in (1, 2, 3):
        ids("x0", d), ids("cx", d), ids("meta", d), ids("tot", d), ids("out", d)
    for name in (("q", 1), ("q", 3), ("q2", 1), ("q2", 3), ("cs",)):
        ids(*name)
    for k in range(1, 8):
        ids("cz", k), ids("bz", k)
        for d in (1, 2, 3):
            ids("bx", k, d)
        if k != 4:
            ids("az", k)
    ids("az", 4, 0), ids("az", 4, 1)
    for k in range(8):
        ids("sib", k)
    return ids


IDS = message_names()


def kernel(q_ref, k_ref, meta_ref, cl_ref, lm_ref, og_ref, ol_ref, kb, qb, mb, clx, clz, pm, amb,
           wbuf, obuf, sbuf, e_acc, p_acc, pos_t, tot, pss, tb, pb, rb, ssem, rsem):
    dp, ix = lax.axis_index("dp"), lax.axis_index("index")
    c, y, x, z = dp % 2, (dp // 2) % NY, (ix % 2) * 2 + dp // (2 * NY), ix // 2

    def dev(xx, yy, zz, cc):
        return ((xx % 2) * NY + yy) * 2 + cc, zz * 2 + xx // 2

    def at_x(d):
        return dev((x + d + NX) % NX, y, z, c)

    def at_y(d):
        return dev(x, (y + d + NY) % NY, z, c)

    def at_z(d):
        return dev(x, y, (z + d + NZ) % NZ, c)

    sibling = dev(x, y, z, 1 - c)
    partners = [at_x(d) for d in (1, 2, 3)] + [at_y(d) for d in (1, 2, 3)] + [at_z(d) for d in range(1, 8)] + [sibling]

    barrier = pltpu.get_barrier_semaphore()
    for partner in partners:
        pl.semaphore_signal(barrier, inc=1, device_id=partner, device_id_type=MESH)

    copies = {}

    def send(name, src, dst, target):
        number = IDS.names[name]
        copy = pltpu.make_async_remote_copy(
            src_ref=src, dst_ref=dst, send_sem=ssem.at[number], recv_sem=rsem.at[number],
            device_id=target, device_id_type=MESH)
        copy.start()
        copies[name] = copy

    def arrived(*name):
        copies[name].wait_recv()

    kf = k_ref[...].astype(F32)
    kn = (kf * lax.rsqrt(jnp.sum(kf * kf, axis=1, keepdims=True) + EPS)).astype(BF16)
    kb[0, 0] = kn[:32]
    kb[0, 1] = kn[32:]
    xf = q_ref[...].astype(F32)
    qb[0] = (xf * lax.rsqrt(jnp.sum(xf * xf, axis=1, keepdims=True) + EPS)).astype(BF16)
    mb[0] = meta_ref[...]
    clx[0] = cl_ref[...]

    pl.semaphore_wait(barrier, len(partners))

    for d in (1, 3, 2):
        send(("x0", d), kb.at[0], kb.at[d], at_x(d))
    send(("bz", 1), kb.at[0, 1], kb.at[unit_of(1) * 4, 1], at_z(1))
    send(("bz", 7), kb.at[0, 1], kb.at[unit_of(7) * 4, 1], at_z(-1))
    send(("q", 1), qb.at[0], qb.at[1], at_y(1))
    send(("q", 3), qb.at[0], qb.at[3], at_y(-1))
    for d in (1, 2, 3):
        send(("meta", d), mb.at[0], mb.at[d], at_y(d))
        send(("cx", d), clx.at[0], clx.at[d], at_x(d))

    for d in (1, 2, 3):
        arrived("cx", d)
    lane = lax.broadcasted_iota(I32, (1, 256), 1)
    row = clx[0]
    for d in (1, 2, 3):
        row = jnp.where(lane // 64 == d, clx[d], row)
    clz[0, 0] = row
    for k in range(1, 8):
        send(("cz", k), clz.at[0, 0], clz.at[0, k], at_z(k))

    for d in (1, 2, 3):
        arrived("x0", d)
    send(("az", 1), kb.at[0:4, 0], kb.at[pl.ds(unit_of(1) * 4, 4), 0], at_z(1))
    send(("az", 7), kb.at[0:4, 0], kb.at[pl.ds(unit_of(7) * 4, 4), 0], at_z(-1))
    send(("sib", 0), kb.at[0:4], kb.at[pl.ds(sibling_unit(0) * 4, 4)], sibling)

    def a_half(k):
        return kb.at[pl.ds(unit_of(k) * 4, 4), 0]

    def b_half(k, j):
        return kb.at[unit_of(k) * 4 + j, 1]

    def forward(r):
        ks = (r, 8 - r) if r < 4 else (4,)
        for k in ks:
            arrived("bz", k)
            if k < 4:
                send(("bz", k + 1), b_half(k, 0), b_half(k + 1, 0), at_z(1))
            elif k > 5:
                send(("bz", k - 1), b_half(k, 0), b_half(k - 1, 0), at_z(-1))
            send(("bx", k, 1), b_half(k, 0), b_half(k, 1), at_x(1))
            send(("bx", k, 3), b_half(k, 0), b_half(k, 3), at_x(-1))
        if r < 4:
            arrived("az", r)
            if r < 3:
                send(("az", r + 1), a_half(r), a_half(r + 1), at_z(1))
            else:
                send(("az", 4, 0), kb.at[pl.ds(unit_of(3) * 4, 2), 0], kb.at[pl.ds(unit_of(4) * 4, 2), 0], at_z(1))
            arrived("az", 8 - r)
            if r < 3:
                send(("az", 7 - r), a_half(8 - r), a_half(7 - r), at_z(-1))
            else:
                send(("az", 4, 1), kb.at[pl.ds(unit_of(5) * 4 + 2, 2), 0],
                     kb.at[pl.ds(unit_of(4) * 4 + 2, 2), 0], at_z(-1))
        else:
            arrived("az", 4, 0)
            arrived("az", 4, 1)
        for k in ks:
            arrived("bx", k, 1)
            arrived("bx", k, 3)
            if k % 2 == 0:
                send(("bx", k, 2), b_half(k, 1), b_half(k, 2), at_x(1))
            else:
                send(("bx", k, 2), b_half(k, 3), b_half(k, 2), at_x(-1))

    def share(r):
        for k in (r, 8 - r) if r < 4 else (4,):
            arrived("bx", k, 2)
            send(("sib", k), kb.at[pl.ds(unit_of(k) * 4, 4)], kb.at[pl.ds(sibling_unit(k) * 4, 4)], sibling)

    def queries_on():
        arrived("q", 1)
        send(("q2", 1), qb.at[1, 0:64], qb.at[2, 0:64], at_y(1))
        arrived("q", 3)
        send(("q2", 3), qb.at[3, 64:128], qb.at[2, 64:128], at_y(-1))

    def prepare():
        for k in range(1, 8):
            arrived("cz", k)
        send(("cs",), clz.at[0], clz.at[1], sibling)
        pm[...] = jnp.zeros_like(pm)
        for d in range(4):
            if d:
                arrived("meta", d)
            pm[d:d + 1, :] = mb[d, :, 0:256].astype(F32)
            pos = jnp.broadcast_to(mb[d, :, 256:384].astype(F32), (128, 128))
            pos_t[d * 128:(d + 1) * 128, :] = pos.T
        tot[...] = jnp.zeros_like(tot)
        pss[...] = jnp.zeros_like(pss)
        arrived("cs")
        arrived("q2", 1)
        arrived("q2", 3)

    def compute(r):
        ks = (r, 8 - r) if 0 < r < 4 else (r,)
        for k in ks:
            arrived("sib", k)
        units = 2 * len(ks)
        first = unit_of(r)

        def unit_step(t, carry):
            if units == 2:
                s, k = t, r
            else:
                s, k = t // 2, r + (t % 2) * (8 - 2 * r)
            keys = kb[pl.ds((first + t) * 4, 4)].reshape(256, 1024)
            sbuf[...] = lax.dot_general(qb[...].reshape(512, 1024), keys, (((1,), (1,)), ((), ())),
                                        preferred_element_type=F32)
            lanes = lax.broadcasted_iota(I32, (1, 256), 1)
            xx = (x - lanes // 64 + NX) % NX
            zz = (z - k + NZ) % NZ
            cc = c + s - 2 * c * s
            rank = (((xx % 2) * NY + y) * 2 + cc) * 16 + zz * 2 + xx // 2
            key_id = (rank * 64 + lanes % 64).astype(F32)
            hot = (lax.broadcasted_iota(I32, (256, 256), 0) == clz[s, k]).astype(F32).astype(BF16)
            amb[...] = lax.dot_general(pm[...].astype(BF16), hot, (((1,), (0,)), ((), ())),
                                       preferred_element_type=F32)
            for b in range(4):
                rows = slice(b * 128, (b + 1) * 128)
                for h in range(2):
                    cols = slice(h * 128, (h + 1) * 128)
                    st = sbuf[rows, cols]
                    is_pos = pos_t[rows, :] == key_id[:, cols]
                    one = jnp.where(is_pos, 1.0, 0.0)
                    w = jnp.exp2(st * EXP2_SCALE) * jnp.maximum(one, amb[b:b + 1, cols])
                    tot[rows, :] += w
                    pss[rows, :] += st * one
                    to = pl.ds(pl.multiple_of(t * 256 + h * 128, 128), 128)
                    wbuf[rows, to] = w.astype(BF16)
                    obuf[rows, to] = one.astype(BF16)
            return carry

        lax.fori_loop(0, units, unit_step, 0)

        def column_step(n, carry):
            cols = pl.ds(pl.multiple_of(n * 256, 256), 256)
            keys = kb[first * 4:(first + units) * 4, :, :, cols].reshape(units * 256, 256)
            e_new = jnp.dot(wbuf[:, 0:units * 256], keys, preferred_element_type=F32)
            p_new = jnp.dot(obuf[:, 0:units * 256], keys, preferred_element_type=F32)
            if r == 0:
                e_acc[:, cols] = e_new
                p_acc[:, cols] = p_new
            else:
                e_acc[:, cols] += e_new
                p_acc[:, cols] += p_new
            return carry

        lax.fori_loop(0, 4, column_step, 0)

    forward(1)
    queries_on()
    forward(2)
    share(1)
    prepare()
    compute(0)
    forward(3)
    share(2)
    compute(1)
    forward(4)
    share(3)
    compute(2)
    share(4)
    compute(3)
    compute(4)

    for b in range(4):
        rows = slice(b * 128, (b + 1) * 128)
        tb[0, b:b + 1, :] = jnp.sum(tot[rows, :].T, axis=0, keepdims=True)
        tb[0, 4 + b:5 + b, :] = jnp.sum(pss[rows, :].T, axis=0, keepdims=True)
    for d in (2, 1, 3):
        send(("tot", d), tb.at[0], tb.at[d], at_y(d))
    for d in (1, 3, 2):
        arrived("tot", d)

    def total_row(b, base):
        row = tb[0, base + b:base + b + 1, :]
        for d in (1, 2, 3):
            i = base + (b - d) % 4
            row = row + tb[d, i:i + 1, :]
        return row

    def partial_rows(b):
        inverse = (1.0 / jnp.broadcast_to(total_row(b, 0), (128, 128)).T)[:, 0:1]
        rows = slice(b * 128, (b + 1) * 128)
        return e_acc[rows, :] * inverse - p_acc[rows, :]

    for b in (2, 1, 3):
        pb[b - 1] = partial_rows(b).astype(BF16)
        send(("out", b), pb.at[b - 1], rb.at[b - 1], at_y(-b))
    ol_ref[...] = jnp.log(total_row(0, 0)) - total_row(0, 4) * 10.0
    og_ref[...] = partial_rows(0)
    for b in (1, 3, 2):
        arrived("out", b)
    direction = og_ref[...] + ((rb[0].astype(F32) + rb[1].astype(F32)) + rb[2].astype(F32))
    scale = (jnp.broadcast_to(lm_ref[...], (128, 128)).T)[:, 0:1] * 10.0
    xf = q_ref[...].astype(F32)
    q_scale = lax.rsqrt(jnp.sum(xf * xf, axis=1, keepdims=True) + EPS)
    g = direction * scale
    projection = jnp.sum(xf * g, axis=1, keepdims=True)
    og_ref[...] = q_scale * g - (q_scale * q_scale * q_scale * projection) * xf
    for copy in copies.values():
        copy.wait_send()


def body(queries, keys, pattern, clusters, positives, loss_multiplier):
    meta = jnp.concatenate([pattern.reshape(1, 256), positives.reshape(1, 128)], axis=1)
    ids = jnp.tile(clusters.reshape(1, 64), (1, 4))
    vmem = pl.BlockSpec(memory_space=pltpu.VMEM)
    count = len(IDS.names)
    grad, loss = pl.pallas_call(
        kernel,
        out_shape=(jax.ShapeDtypeStruct((128, 1024), F32), jax.ShapeDtypeStruct((1, 128), F32)),
        in_specs=[vmem] * 5,
        out_specs=(vmem, vmem),
        scratch_shapes=[
            pltpu.VMEM((64, 2, 32, 1024), BF16),
            pltpu.VMEM((4, 128, 1024), BF16),
            pltpu.VMEM((4, 1, 384), I32),
            pltpu.VMEM((4, 1, 256), I32),
            pltpu.VMEM((2, 8, 1, 256), I32),
            pltpu.VMEM((8, 256), F32),
            pltpu.VMEM((8, 256), F32),
            pltpu.VMEM((512, 1024), BF16),
            pltpu.VMEM((512, 1024), BF16),
            pltpu.VMEM((512, 256), F32),
            pltpu.VMEM((512, 1024), F32),
            pltpu.VMEM((512, 1024), F32),
            pltpu.VMEM((512, 128), F32),
            pltpu.VMEM((512, 128), F32),
            pltpu.VMEM((512, 128), F32),
            pltpu.VMEM((4, 8, 128), F32),
            pltpu.VMEM((3, 128, 1024), BF16),
            pltpu.VMEM((3, 128, 1024), BF16),
            pltpu.SemaphoreType.DMA((count,)),
            pltpu.SemaphoreType.DMA((count,)),
        ],
        compiler_params=pltpu.CompilerParams(
            collective_id=0, has_side_effects=True, vmem_limit_bytes=50 * 1024 * 1024),
        name="contrastive",
    )(queries, keys, meta, ids, loss_multiplier.reshape(1, 128))
    return grad, loss.reshape(128)


def solution(mesh):
    rows, flat = P(("dp", "index"), None), P(("dp", "index"))
    return jax.shard_map(
        body, mesh=mesh, in_specs=(rows, rows, rows, flat, flat, flat), out_specs=(rows, flat), check_vma=False)
```

time: 378 us -> 90.1 us (0.24)
  blocking collectives: 95.7 us -> 0 us
  waiting for transfers between devices: 85.5 us -> 0 us
  Pallas kernels: 0 us -> 84.1 us
  matrix products: 82.8 us -> 0 us
  starting transfers between devices: 56 us -> 0 us
  other arithmetic: 22.1 us -> 0.01 us
  between operations: 14.6 us -> 0.66 us
  local copies, waits for them, and re-layouts: 17.1 us -> 5.13 us
    pallas_call x0 -> x1, Pallas kernels: none -> 84.1 us  [body(): pl.pallas_call(kernel, out_shape=(jax.ShapeDtypeStruct((128, 1024), F32),...]
    dot_general x33 -> x0, matrix products: 82.8 us -> none  [the longest x16 70.2 us: tile_weights(): lax.dot_general(key_tile, gathered, (((1,), (1,)), ((), ())), preferred_e...]
    reduce_scatter x2 -> x0, waiting for transfers between devices: 81.3 us -> none  [the longest x1 78.3 us: body(): lax.psum_scatter(selected_lower.astype(jnp.float32), 'dp', scatter_dimens...]
    unnamed x1 -> x0, blocking collectives: 58.4 us -> none
    ppermute x30 -> x0, starting transfers between devices: 55.9 us -> none  [shifted(): return lax.ppermute(value, axis, pairs)]
    all_gather x2 -> x0, blocking collectives: 37.3 us -> none  [the longest x1 21.1 us: body(): lax.all_gather(id_pair, 'dp', axis=0, tiled=True)]
    gather x1 -> x0, local copies, waits for them, and re-layouts: 9.68 us -> none  [body(): picked = flat_keys[slots * tile_rows + within]]
    reduce_sum x19 -> x0, other arithmetic: 8.84 us -> none  [the longest x16 5.26 us: tile_weights(): jnp.sum(inner_product_matrix * is_positive, axis=0)]
  transfers between devices with their start and end apart: 33 -> 0, of which waited for: 4 -> 0; matrix products, arithmetic and copies ran while one was open for 26% -> 0% of each run, Pallas kernels for 0% -> 0%
where the time goes in v1:
time: 90.1 us; the launch traced here: 89.9 us
  Pallas kernels  84.1 us (93%)
  local copies, waits for them, and re-layouts  5.13 us (6%)
    pallas_call x1, Pallas kernels, body(): pl.pallas_call(kernel, out_shape=(jax.ShapeDtypeStruct((128, 1024), F32),...  84.1 us
    unnamed x14, local copies, waits for them, and re-layouts  5.05 us

profile of v1, /device:TPU:1, one launch (start us, length us, event | category | flops | bytes accessed | tf_op | source)
XLA Modules:
  0.0 89.9 jit_solution(18348693161908189267)
XLA Ops:
  0.6 0.0 copy-start.3
  0.6 0.0 copy-start.5
  0.7 0.7 copy-done.3
  1.3 0.0 copy-done.5
  1.3 0.0 copy-start.4
  1.3 0.7 copy-done.4
  2.0 0.0 copy-start.2
  2.0 0.1 tile.9.cl_ref
  2.1 0.6 copy-done.2
  2.6 0.0 copy-start
  2.6 0.9 %copy-done = bf16[128,1024]{1,0:T(8,128)(2,1)S(1)} copy-done((bf16[128,1024]{1,0:T(8,128)(2,1)S(1)}, bf16[128,1024]{1,0:T(8,128)(2,1)}, u32[]{:S(2)}) %copy-start) | copy-done | bytes 262168
  3.6 0.0 copy-start.1
  3.6 0.9 %copy-done.1 = bf16[64,1024]{1,0:T(8,128)(2,1)S(1)} copy-done((bf16[64,1024]{1,0:T(8,128)(2,1)S(1)}, bf16[64,1024]{1,0:T(8,128)(2,1)}, u32[]{:S(2)}) %copy-start.1) | copy-done | bytes 131096
  4.5 84.1 %contrastive.1 = (f32[128,1024]{1,0:T(8,128)S(1)}, f32[1,128]{1,0:T(1,128)S(1)}) custom-call(bf16[128,1024]{1,0:T(8,128)(2,1)S(1)} %copy-done, bf16[64,1024]{1,0:T(8,128)(2,1)S(1)} %copy-done.1, s32[1,384]{1,0:T(1,128)S(1)} %pad_add_fusion.meta_ref, s32[1,256]{1,0:T(1,128)S(1)} %tile.9.cl_ref, f32[1,128]{1,0:T(1,128)S(1)} %bitcast.3), custom_call_target="tpu_custom_call" | custom-call | tf_op jit(solution)/shard_map/contrastive/pallas_call | solution.py:316
  88.6 0.8 copy.10
  89.4 0.5 copy.11
  (2 shorter events, 0.0 us)
Async XLA Ops:
  0.6 0.7 copy-start.3
  0.6 0.7 copy-start.5
  1.3 0.7 copy-start.4
  2.0 0.7 copy-start.2
  2.6 0.9 %copy-start = (bf16[128,1024]{1,0:T(8,128)(2,1)S(1)}, bf16[128,1024]{1,0:T(8,128)(2,1)}, u32[]{:S(2)}) copy-start(bf16[128,1024]{1,0:T(8,128)(2,1)} %q_ref.1) | copy-start | bytes 786436
  3.6 0.9 %copy-start.1 = (bf16[64,1024]{1,0:T(8,128)(2,1)S(1)}, bf16[64,1024]{1,0:T(8,128)(2,1)}, u32[]{:S(2)}) copy-start(bf16[64,1024]{1,0:T(8,128)(2,1)} %k_ref.1) | copy-start | bytes 393220

commit v2 on v1

v2 whole, which is shorter than its diff:
```python
import functools
import math

import jax
import jax.numpy as jnp
from jax import lax
from jax.experimental import pallas as pl
from jax.experimental.pallas import tpu as pltpu
from jax.sharding import PartitionSpec as P

MESH = pl.DeviceIdType.MESH
EPS = 1e-06
NX, NY, NZ = 4, 4, 8
EXP2_SCALE = 10.0 * math.log2(math.e)
F32, BF16, I32 = jnp.float32, jnp.bfloat16, jnp.int32


def unit_of(k):
    if k == 0:
        return 0
    if k == 4:
        return 14
    return 2 + 4 * (k - 1) if k < 4 else 2 + 4 * (7 - k) + 1


def sibling_unit(k):
    return unit_of(k) + (1 if k in (0, 4) else 2)


class Ids:
    def __init__(self):
        self.names = {}

    def __call__(self, *name):
        return self.names.setdefault(name, len(self.names))


def message_names():
    ids = Ids()
    for d in (1, 2, 3):
        ids("xa", d), ids("xb", d), ids("cx", d), ids("meta", d), ids("tot", d), ids("out", d)
    for name in (("q", 1), ("q", 3), ("q2", 1), ("q2", 3), ("cs",)):
        ids(*name)
    for k in range(1, 8):
        ids("cz", k), ids("f", k)
        for d in (1, 2, 3):
            ids("bx", k, d), ids("g", k, d)
    for k in range(8):
        ids("sib", k)
    return ids


IDS = message_names()


def kernel(q_ref, k_ref, pat_ref, cl_ref, pos_ref, lm_ref, og_ref, ol_ref, kin, qin, clv, lmv, kb, qb, mb, clx, clz,
           pm, amb, wbuf, obuf, sbuf, e_acc, p_acc, pos_t, tot, pss, tb, pb, rb, lsem, ssem, rsem):
    dp, ix = lax.axis_index("dp"), lax.axis_index("index")
    c, y, x, z = dp % 2, (dp // 2) % NY, (ix % 2) * 2 + dp // (2 * NY), ix // 2

    def dev(xx, yy, zz, cc):
        return ((xx % 2) * NY + yy) * 2 + cc, zz * 2 + xx // 2

    def at_x(d):
        return dev((x + d + NX) % NX, y, z, c)

    def at_y(d):
        return dev(x, (y + d + NY) % NY, z, c)

    def at_z(d):
        return dev(x, y, (z + d + NZ) % NZ, c)

    sibling = dev(x, y, z, 1 - c)
    partners = [at_x(d) for d in (1, 2, 3)] + [at_y(d) for d in (1, 2, 3)] + [at_z(d) for d in range(1, 8)] + [sibling]

    barrier = pltpu.get_barrier_semaphore()
    for partner in partners:
        pl.semaphore_signal(barrier, inc=1, device_id=partner, device_id_type=MESH)

    copies = {}

    def send(name, src, dst, target):
        number = IDS.names[name]
        copy = pltpu.make_async_remote_copy(
            src_ref=src, dst_ref=dst, send_sem=ssem.at[number], recv_sem=rsem.at[number],
            device_id=target, device_id_type=MESH)
        copy.start()
        copies[name] = copy

    def arrived(*name):
        copies[name].wait_recv()

    loads = [
        pltpu.make_async_copy(k_ref, kin, lsem.at[0]),
        pltpu.make_async_copy(q_ref, qin, lsem.at[1]),
        pltpu.make_async_copy(pat_ref, mb.at[0, :, 0:256], lsem.at[2]),
        pltpu.make_async_copy(pos_ref, mb.at[0, :, 256:384], lsem.at[3]),
        pltpu.make_async_copy(cl_ref, clv, lsem.at[4]),
        pltpu.make_async_copy(lm_ref, lmv, lsem.at[5]),
    ]
    for load in loads:
        load.start()
    loads[0].wait()
    kf = kin[...].astype(F32)
    kn = (kf * lax.rsqrt(jnp.sum(kf * kf, axis=1, keepdims=True) + EPS)).astype(BF16)
    kb[0, 0] = kn[:32]
    kb[0, 1] = kn[32:]
    pl.semaphore_wait(barrier, len(partners))

    def g_half(k, j):
        return kb.at[unit_of(k) * 4 + j, 0]

    def send_g(k, j, source):
        send(("g", k, j), source, g_half(k, j), at_z(1 if k < 4 else -1))

    def send_f(k, source):
        send(("f", k), source, kb.at[unit_of(k) * 4], at_z(1 if k <= 4 else -1))

    def b_half(k, j):
        return kb.at[unit_of(k) * 4 + j, 1]

    for d in (1, 3, 2):
        send(("xa", d), kb.at[0, 0], kb.at[d, 0], at_x(d))
    send_f(1, kb.at[0])
    send_f(7, kb.at[0])
    loads[1].wait()
    xf = qin[...].astype(F32)
    qb[0] = (xf * lax.rsqrt(jnp.sum(xf * xf, axis=1, keepdims=True) + EPS)).astype(BF16)
    send(("q", 1), qb.at[0], qb.at[1], at_y(1))
    send(("q", 3), qb.at[0], qb.at[3], at_y(-1))
    for load in loads[2:]:
        load.wait()
    for j in (1, 3, 2):
        arrived("xa", j)
        send_g(1, j, kb.at[j, 0])
        send_g(7, j, kb.at[j, 0])
    for d in (1, 3, 2):
        send(("xb", d), kb.at[0, 1], kb.at[d, 1], at_x(d))
    spread = lax.broadcasted_iota(I32, (64, 256), 0) == lax.broadcasted_iota(I32, (64, 256), 1) % 64
    clx[0] = jnp.dot(jnp.broadcast_to(clv[...].astype(F32), (8, 64)).astype(BF16), spread.astype(F32).astype(BF16),
                     preferred_element_type=F32)[0:1].astype(I32)
    for d in (1, 2, 3):
        send(("meta", d), mb.at[0], mb.at[d], at_y(d))
        send(("cx", d), clx.at[0], clx.at[d], at_x(d))

    def cluster_rows():
        for d in (1, 2, 3):
            arrived("cx", d)
        lane = lax.broadcasted_iota(I32, (1, 256), 1)
        row = clx[0]
        for d in (1, 2, 3):
            row = jnp.where(lane // 64 == d, clx[d], row)
        clz[0, 0] = row
        for k in range(1, 8):
            send(("cz", k), clz.at[0, 0], clz.at[0, k], at_z(k))

    def whole(k):
        arrived("f", k)
        if k < 4:
            send_f(k + 1, kb.at[unit_of(k) * 4])
        elif k > 5:
            send_f(k - 1, kb.at[unit_of(k) * 4])
        for d in (1, 3, 2):
            send(("bx", k, d), b_half(k, 0), b_half(k, d), at_x(d))

    def half(k, j):
        arrived("g", k, j)
        if k < 3:
            send_g(k + 1, j, g_half(k, j))
        elif k > 4:
            send_g(k - 1, j, g_half(k, j))

    def events(r):
        ks = (r, 8 - r) if r < 4 else (4,)
        steps = [functools.partial(whole, k) for k in ks]
        return steps + [functools.partial(half, k, j) for j in (1, 3, 2) for k in ks]

    def share(r):
        for k in (r, 8 - r) if 0 < r < 4 else (r,):
            for d in (1, 3, 2):
                if k:
                    arrived("bx", k, d)
                else:
                    arrived("xb", d)
            send(("sib", k), kb.at[pl.ds(unit_of(k) * 4, 4)], kb.at[pl.ds(sibling_unit(k) * 4, 4)], sibling)

    def queries_on():
        arrived("q", 1)
        send(("q2", 1), qb.at[1, 0:64], qb.at[2, 0:64], at_y(1))
        arrived("q", 3)
        send(("q2", 3), qb.at[3, 64:128], qb.at[2, 64:128], at_y(-1))

    def prepare():
        for k in range(1, 8):
            arrived("cz", k)
        send(("cs",), clz.at[0], clz.at[1], sibling)
        pm[...] = jnp.zeros_like(pm)
        for d in range(4):
            if d:
                arrived("meta", d)
            pm[d:d + 1, :] = mb[d, :, 0:256].astype(F32)
            pos = jnp.broadcast_to(mb[d, :, 256:384].astype(F32), (128, 128))
            pos_t[d * 128:(d + 1) * 128, :] = pos.T
        tot[...] = jnp.zeros_like(tot)
        pss[...] = jnp.zeros_like(pss)
        arrived("cs")
        arrived("q2", 1)
        arrived("q2", 3)

    def score(r, t, s, k):
        if s == 1:
            arrived("sib", k)
        unit = unit_of(r) + t
        keys = kb[unit * 4:unit * 4 + 4].reshape(256, 1024)
        sbuf[...] = lax.dot_general(qb[...].reshape(512, 1024), keys, (((1,), (1,)), ((), ())),
                                    preferred_element_type=F32)
        lanes = lax.broadcasted_iota(I32, (1, 256), 1)
        xx = (x - lanes // 64 + NX) % NX
        zz = (z - k + NZ) % NZ
        cc = c + s - 2 * c * s
        rank = (((xx % 2) * NY + y) * 2 + cc) * 16 + zz * 2 + xx // 2
        key_id = (rank * 64 + lanes % 64).astype(F32)
        hot = (lax.broadcasted_iota(I32, (256, 256), 0) == clz[s, k]).astype(F32).astype(BF16)
        amb[...] = lax.dot_general(pm[...].astype(BF16), hot, (((1,), (0,)), ((), ())),
                                   preferred_element_type=F32)
        for b in range(4):
            rows = slice(b * 128, (b + 1) * 128)
            for h in range(2):
                cols = slice(h * 128, (h + 1) * 128)
                st = sbuf[rows, cols]
                is_pos = pos_t[rows, :] == key_id[:, cols]
                one = jnp.where(is_pos, 1.0, 0.0)
                w = jnp.exp2(st * EXP2_SCALE) * jnp.maximum(one, amb[b:b + 1, cols])
                tot[rows, :] += w
                pss[rows, :] += st * one
                to = slice(t * 256 + h * 128, t * 256 + h * 128 + 128)
                wbuf[rows, to] = w.astype(BF16)
                obuf[rows, to] = one.astype(BF16)

    def column(r, units, n):
        first = unit_of(r)
        cols = slice(n * 256, (n + 1) * 256)
        keys = kb[first * 4:(first + units) * 4, :, :, cols].reshape(units * 256, 256)
        e_new = jnp.dot(wbuf[:, 0:units * 256], keys, preferred_element_type=F32)
        p_new = jnp.dot(obuf[:, 0:units * 256], keys, preferred_element_type=F32)
        if r == 0:
            e_acc[:, cols] = e_new
            p_acc[:, cols] = p_new
        else:
            e_acc[:, cols] += e_new
            p_acc[:, cols] += p_new

    def pieces(r):
        ks = (r, 8 - r) if 0 < r < 4 else (r,)
        order = [(s, k) for s in (0, 1) for k in ks]
        steps = [functools.partial(score, r, t, s, k) for t, (s, k) in enumerate(order)]
        return steps + [functools.partial(column, r, len(order), n) for n in range(4)]

    def run(first, second=()):
        first, second = list(first), list(second)
        done = 0
        for i, step in enumerate(first):
            step()
            upto = (i + 1) * len(second) // len(first)
            for other in second[done:upto]:
                other()
            done = upto

    steps = events(1)
    run(steps[:4])
    cluster_rows()
    queries_on()
    run(steps[4:])
    share(0)
    prepare()
    run(events(2), pieces(0))
    share(1)
    run(events(3), pieces(1))
    share(2)
    run(events(4), pieces(2))
    share(3)
    share(4)
    run(pieces(3))
    run(pieces(4))

    for b in range(4):
        rows = slice(b * 128, (b + 1) * 128)
        tb[0, b:b + 1, :] = jnp.sum(tot[rows, :].T, axis=0, keepdims=True)
        tb[0, 4 + b:5 + b, :] = jnp.sum(pss[rows, :].T, axis=0, keepdims=True)
    for d in (2, 1, 3):
        send(("tot", d), tb.at[0], tb.at[d], at_y(d))
    for d in (1, 3, 2):
        arrived("tot", d)

    def total_row(b, base):
        row = tb[0, base + b:base + b + 1, :]
        for d in (1, 2, 3):
            i = base + (b - d) % 4
            row = row + tb[d, i:i + 1, :]
        return row

    def partial_rows(b):
        inverse = (1.0 / jnp.broadcast_to(total_row(b, 0), (128, 128)).T)[:, 0:1]
        rows = slice(b * 128, (b + 1) * 128)
        return e_acc[rows, :] * inverse - p_acc[rows, :]

    for b in (2, 1, 3):
        pb[b - 1] = partial_rows(b).astype(BF16)
        send(("out", b), pb.at[b - 1], rb.at[b - 1], at_y(-b))
    ol_ref[...] = jnp.log(total_row(0, 0)) - total_row(0, 4) * 10.0
    og_ref[...] = partial_rows(0)
    for b in (1, 3, 2):
        arrived("out", b)
    direction = og_ref[...] + ((rb[0].astype(F32) + rb[1].astype(F32)) + rb[2].astype(F32))
    scale = (jnp.broadcast_to(lmv[...], (128, 128)).T)[:, 0:1] * 10.0
    xf = qin[...].astype(F32)
    q_scale = lax.rsqrt(jnp.sum(xf * xf, axis=1, keepdims=True) + EPS)
    g = direction * scale
    projection = jnp.sum(xf * g, axis=1, keepdims=True)
    og_ref[...] = q_scale * g - (q_scale * q_scale * q_scale * projection) * xf
    for copy in copies.values():
        copy.wait_send()


def body(queries, keys, pattern, clusters, positives, loss_multiplier):
    hbm = pl.BlockSpec(memory_space=pltpu.HBM)
    vmem = pl.BlockSpec(memory_space=pltpu.VMEM)
    count = len(IDS.names)
    grad, loss = pl.pallas_call(
        kernel,
        out_shape=(jax.ShapeDtypeStruct((128, 1024), F32), jax.ShapeDtypeStruct((1, 128), F32)),
        in_specs=[hbm] * 6,
        out_specs=(vmem, vmem),
        scratch_shapes=[
            pltpu.VMEM((64, 1024), BF16),
            pltpu.VMEM((128, 1024), BF16),
            pltpu.VMEM((1, 64), I32),
            pltpu.VMEM((1, 128), F32),
            pltpu.VMEM((64, 2, 32, 1024), BF16),
            pltpu.VMEM((4, 128, 1024), BF16),
            pltpu.VMEM((4, 1, 384), I32),
            pltpu.VMEM((4, 1, 256), I32),
            pltpu.VMEM((2, 8, 1, 256), I32),
            pltpu.VMEM((8, 256), F32),
            pltpu.VMEM((8, 256), F32),
            pltpu.VMEM((512, 1024), BF16),
            pltpu.VMEM((512, 1024), BF16),
            pltpu.VMEM((512, 256), F32),
            pltpu.VMEM((512, 1024), F32),
            pltpu.VMEM((512, 1024), F32),
            pltpu.VMEM((512, 128), F32),
            pltpu.VMEM((512, 128), F32),
            pltpu.VMEM((512, 128), F32),
            pltpu.VMEM((4, 8, 128), F32),
            pltpu.VMEM((3, 128, 1024), BF16),
            pltpu.VMEM((3, 128, 1024), BF16),
            pltpu.SemaphoreType.DMA((6,)),
            pltpu.SemaphoreType.DMA((count,)),
            pltpu.SemaphoreType.DMA((count,)),
        ],
        compiler_params=pltpu.CompilerParams(
            collective_id=0, has_side_effects=True, vmem_limit_bytes=63 * 1024 * 1024 + 768 * 1024),
        name="contrastive",
    )(queries, keys, pattern, clusters.reshape(1, 64), positives.reshape(1, 128), loss_multiplier.reshape(1, 128))
    return grad, loss.reshape(128)


def solution(mesh):
    rows, flat = P(("dp", "index"), None), P(("dp", "index"))
    return jax.shard_map(
        body, mesh=mesh, in_specs=(rows, rows, rows, flat, flat, flat), out_specs=(rows, flat), check_vma=False)
```

time: 90.1 us -> 76.1 us (0.84)
  Pallas kernels: 84.1 us -> 72.9 us
  local copies, waits for them, and re-layouts: 5.13 us -> 2.4 us
    pallas_call x1, Pallas kernels: 84.1 us -> 72.9 us  [body(): pl.pallas_call(kernel, out_shape=(jax.ShapeDtypeStruct((128, 1024), F32),...]
    unnamed x14 -> x4, local copies, waits for them, and re-layouts: 5.05 us -> 2.4 us
where the time goes in v2:
time: 76.1 us; the launch traced here: 76 us
  Pallas kernels  72.9 us (96%)
  local copies, waits for them, and re-layouts  2.4 us (3%)
    pallas_call x1, Pallas kernels, body(): pl.pallas_call(kernel, out_shape=(jax.ShapeDtypeStruct((128, 1024), F32),...  72.9 us
    unnamed x4, local copies, waits for them, and re-layouts  2.4 us

profile of v2, /device:TPU:1, one launch (start us, length us, event | category | flops | bytes accessed | tf_op | source)
XLA Modules:
  0.0 76.0 jit_solution(7104849406733062327)
XLA Ops:
  0.6 72.9 %contrastive.1 = (f32[128,1024]{1,0:T(8,128)}, f32[1,128]{1,0:T(1,128)}) custom-call(bf16[128,1024]{1,0:T(8,128)(2,1)} %q_ref.1, bf16[64,1024]{1,0:T(8,128)(2,1)} %k_ref.1, s32[1,256]{1,0:T(1,128)} %pat_ref.1, s32[1,64]{1,0:T(1,128)} %bitcast.4, s32[1,128]{1,0:T(1,128)} %bitcast.5, f32[1,128]{1,0:T(1,128)} %bitcast.6), custom_call_target="tpu_custom_call" | custom-call | tf_op jit(solution)/shard_map/contrastive/pallas_call | solution.py:329
  73.5 0.0 copy-start
  73.5 1.9 %copy.10 = f32[128,1024]{1,0:T(8,128)} copy(f32[128,1024]{1,0:T(8,128)} %get-tuple-element.8) | data formatting | bytes 1048576
  75.4 0.0 copy-done
  75.4 0.5 copy.11
Async XLA Ops:
  73.5 1.9 %copy-start = (f32[1,128]{1,0:T(1,128)S(1)}, f32[1,128]{1,0:T(1,128)}, u32[]{:S(2)}) copy-start(f32[1,128]{1,0:T(1,128)} %get-tuple-element.5) | copy-start | bytes 1540

commit v3 on v2

--- a/solution.py
+++ b/solution.py
@@ -38,7 +38,7 @@
 def message_names():
     ids = Ids()
     for d in (1, 2, 3):
-        ids("xa", d), ids("xb", d), ids("cx", d), ids("meta", d), ids("tot", d), ids("out", d)
+        ids("xa", d), ids("xb", d), ids("cx", d), ids("meta", d), ids("tot", d)
     for name in (("q", 1), ("q", 3), ("q2", 1), ("q2", 3), ("cs",)):
         ids(*name)
     for k in range(1, 8):
@@ -47,14 +47,18 @@
             ids("bx", k, d), ids("g", k, d)
     for k in range(8):
         ids("sib", k)
+    for n in range(4):
+        for h in (0, 1):
+            ids("rel", n, h), ids("out", 1, n, h), ids("out", 3, n, h)
     return ids
 
 
 IDS = message_names()
+STAGES = (((0,),), ((1, 7),), ((2, 6),), ((3, 5),), ((4,),))
 
 
 def kernel(q_ref, k_ref, pat_ref, cl_ref, pos_ref, lm_ref, og_ref, ol_ref, kin, qin, clv, lmv, kb, qb, mb, clx, clz,
-           pm, amb, wbuf, obuf, sbuf, e_acc, p_acc, pos_t, tot, pss, tb, pb, rb, lsem, ssem, rsem):
+           pm, amb, wbuf, obuf, sbuf, e_acc, p_acc, pos_t, tot, pss, tb, pb, rb, rl, lsem, ssem, rsem):
     dp, ix = lax.axis_index("dp"), lax.axis_index("index")
     c, y, x, z = dp % 2, (dp // 2) % NY, (ix % 2) * 2 + dp // (2 * NY), ix // 2
 
@@ -100,11 +104,17 @@
     ]
     for load in loads:
         load.start()
-    loads[0].wait()
+    for load in loads:
+        load.wait()
+    spread = lax.broadcasted_iota(I32, (64, 256), 0) == lax.broadcasted_iota(I32, (64, 256), 1) % 64
+    clx[0] = jnp.dot(jnp.broadcast_to(clv[...].astype(F32), (8, 64)).astype(BF16), spread.astype(F32).astype(BF16),
+                     preferred_element_type=F32)[0:1].astype(I32)
     kf = kin[...].astype(F32)
     kn = (kf * lax.rsqrt(jnp.sum(kf * kf, axis=1, keepdims=True) + EPS)).astype(BF16)
     kb[0, 0] = kn[:32]
     kb[0, 1] = kn[32:]
+    xf = qin[...].astype(F32)
+    qb[0] = (xf * lax.rsqrt(jnp.sum(xf * xf, axis=1, keepdims=True) + EPS)).astype(BF16)
     pl.semaphore_wait(barrier, len(partners))
 
     def g_half(k, j):
@@ -120,28 +130,19 @@
         return kb.at[unit_of(k) * 4 + j, 1]
 
     for d in (1, 3, 2):
+        send(("cx", d), clx.at[0], clx.at[d], at_x(d))
         send(("xa", d), kb.at[0, 0], kb.at[d, 0], at_x(d))
     send_f(1, kb.at[0])
     send_f(7, kb.at[0])
-    loads[1].wait()
-    xf = qin[...].astype(F32)
-    qb[0] = (xf * lax.rsqrt(jnp.sum(xf * xf, axis=1, keepdims=True) + EPS)).astype(BF16)
     send(("q", 1), qb.at[0], qb.at[1], at_y(1))
     send(("q", 3), qb.at[0], qb.at[3], at_y(-1))
-    for load in loads[2:]:
-        load.wait()
-    for j in (1, 3, 2):
+    for d in (1, 2, 3):
+        send(("meta", d), mb.at[0], mb.at[d], at_y(d))
+
+    def near(j):
         arrived("xa", j)
         send_g(1, j, kb.at[j, 0])
         send_g(7, j, kb.at[j, 0])
-    for d in (1, 3, 2):
-        send(("xb", d), kb.at[0, 1], kb.at[d, 1], at_x(d))
-    spread = lax.broadcasted_iota(I32, (64, 256), 0) == lax.broadcasted_iota(I32, (64, 256), 1) % 64
-    clx[0] = jnp.dot(jnp.broadcast_to(clv[...].astype(F32), (8, 64)).astype(BF16), spread.astype(F32).astype(BF16),
-                     preferred_element_type=F32)[0:1].astype(I32)
-    for d in (1, 2, 3):
-        send(("meta", d), mb.at[0], mb.at[d], at_y(d))
-        send(("cx", d), clx.at[0], clx.at[d], at_x(d))
 
     def cluster_rows():
         for d in (1, 2, 3):
@@ -169,11 +170,6 @@
             send_g(k + 1, j, g_half(k, j))
         elif k > 4:
             send_g(k - 1, j, g_half(k, j))
-
-    def events(r):
-        ks = (r, 8 - r) if r < 4 else (4,)
-        steps = [functools.partial(whole, k) for k in ks]
-        return steps + [functools.partial(half, k, j) for j in (1, 3, 2) for k in ks]
 
     def share(r):
         for k in (r, 8 - r) if 0 < r < 4 else (r,):
@@ -207,10 +203,10 @@
         arrived("q2", 1)
         arrived("q2", 3)
 
-    def score(r, t, s, k):
+    def score(first, t, s, k):
         if s == 1:
             arrived("sib", k)
-        unit = unit_of(r) + t
+        unit = first + t
         keys = kb[unit * 4:unit * 4 + 4].reshape(256, 1024)
         sbuf[...] = lax.dot_general(qb[...].reshape(512, 1024), keys, (((1,), (1,)), ((), ())),
                                     preferred_element_type=F32)
@@ -237,24 +233,29 @@
                 wbuf[rows, to] = w.astype(BF16)
                 obuf[rows, to] = one.astype(BF16)
 
-    def column(r, units, n):
-        first = unit_of(r)
+    def column(first, units, n):
         cols = slice(n * 256, (n + 1) * 256)
         keys = kb[first * 4:(first + units) * 4, :, :, cols].reshape(units * 256, 256)
         e_new = jnp.dot(wbuf[:, 0:units * 256], keys, preferred_element_type=F32)
         p_new = jnp.dot(obuf[:, 0:units * 256], keys, preferred_element_type=F32)
-        if r == 0:
+        if first == 0:
             e_acc[:, cols] = e_new
             p_acc[:, cols] = p_new
         else:
             e_acc[:, cols] += e_new
             p_acc[:, cols] += p_new
 
-    def pieces(r):
-        ks = (r, 8 - r) if 0 < r < 4 else (r,)
-        order = [(s, k) for s in (0, 1) for k in ks]
-        steps = [functools.partial(score, r, t, s, k) for t, (s, k) in enumerate(order)]
-        return steps + [functools.partial(column, r, len(order), n) for n in range(4)]
+    def scores(stage):
+        ks = STAGES[stage]
+        steps = []
+        for part in ks:
+            for s in (0, 1):
+                steps += [functools.partial(score, unit_of(ks[0][0]), len(steps) + i, s, k) for i, k in enumerate(part)]
+        return steps
+
+    def columns(stage):
+        units = 2 * sum(len(part) for part in STAGES[stage])
+        return [functools.partial(column, unit_of(STAGES[stage][0][0]), units, n) for n in range(4)]
 
     def run(first, second=()):
         first, second = list(first), list(second)
@@ -266,22 +267,37 @@
                 other()
             done = upto
 
-    steps = events(1)
-    run(steps[:4])
+    def wholes(r):
+        return [functools.partial(whole, k) for k in ((r, 8 - r) if r < 4 else (4,))]
+
+    def halves(r, js=(1, 3, 2)):
+        return [functools.partial(half, k, j) for j in js for k in ((r, 8 - r) if r < 4 else (4,))]
+
+    def events(r):
+        return wholes(r) + halves(r)
+
     cluster_rows()
+    near(1)
+    near(3)
+    near(2)
+    for d in (1, 3, 2):
+        send(("xb", d), kb.at[0, 1], kb.at[d, 1], at_x(d))
+    run(wholes(1) + halves(1, (1,)))
     queries_on()
-    run(steps[4:])
+    run(halves(1, (3, 2)))
     share(0)
     prepare()
-    run(events(2), pieces(0))
+    run(events(2), scores(0) + columns(0))
     share(1)
-    run(events(3), pieces(1))
+    run(events(3), scores(1) + columns(1))
     share(2)
-    run(events(4), pieces(2))
+    run(wholes(4), scores(2))
+    run(halves(4, (1,)), columns(2))
     share(3)
+    run(halves(4, (3, 2)), scores(3))
     share(4)
-    run(pieces(3))
-    run(pieces(4))
+    run(columns(3))
+    run(scores(4))
 
     for b in range(4):
         rows = slice(b * 128, (b + 1) * 128)
@@ -289,8 +305,6 @@
         tb[0, 4 + b:5 + b, :] = jnp.sum(pss[rows, :].T, axis=0, keepdims=True)
     for d in (2, 1, 3):
         send(("tot", d), tb.at[0], tb.at[d], at_y(d))
-    for d in (1, 3, 2):
-        arrived("tot", d)
 
     def total_row(b, base):
         row = tb[0, base + b:base + b + 1, :]
@@ -299,25 +313,65 @@
             row = row + tb[d, i:i + 1, :]
         return row
 
-    def partial_rows(b):
-        inverse = (1.0 / jnp.broadcast_to(total_row(b, 0), (128, 128)).T)[:, 0:1]
+    def partial_rows(b, cols):
         rows = slice(b * 128, (b + 1) * 128)
-        return e_acc[rows, :] * inverse - p_acc[rows, :]
-
-    for b in (2, 1, 3):
-        pb[b - 1] = partial_rows(b).astype(BF16)
-        send(("out", b), pb.at[b - 1], rb.at[b - 1], at_y(-b))
+        inverse = jnp.concatenate([tot[rows, :]] * 2, axis=1)
+        return e_acc[rows, cols] * inverse - p_acc[rows, cols]
+
+    upper, lower = slice(0, 64), slice(64, 128)
+
+    def leave(n):
+        cols = slice(n * 256, (n + 1) * 256)
+        pb[2, n] = partial_rows(2, cols).astype(BF16)
+        send(("rel", n, 0), pb.at[2, n, upper], rl.at[0, n], at_y(-1))
+        send(("rel", n, 1), pb.at[2, n, lower], rl.at[1, n], at_y(1))
+        near_y = partial_rows(1, cols)
+        pb[0, n, lower] = near_y[lower].astype(BF16)
+        send(("out", 1, n, 1), pb.at[0, n, lower], rb.at[0, n, lower], at_y(-1))
+        far_y = partial_rows(3, cols)
+        pb[1, n, upper] = far_y[upper].astype(BF16)
+        send(("out", 3, n, 0), pb.at[1, n, upper], rb.at[1, n, upper], at_y(1))
+
+    def pass_on(n):
+        cols = slice(n * 256, (n + 1) * 256)
+        arrived("rel", n, 0)
+        pb[0, n, upper] = (partial_rows(1, cols)[upper] + rl[0, n].astype(F32)).astype(BF16)
+        send(("out", 1, n, 0), pb.at[0, n, upper], rb.at[0, n, upper], at_y(-1))
+        arrived("rel", n, 1)
+        pb[1, n, lower] = (partial_rows(3, cols)[lower] + rl[1, n].astype(F32)).astype(BF16)
+        send(("out", 3, n, 1), pb.at[1, n, lower], rb.at[1, n, lower], at_y(1))
+
+    final = columns(4)
+    run(final[:2])
+    for d in (1, 3, 2):
+        arrived("tot", d)
+    for b in (2, 1, 3, 0):
+        tot[b * 128:(b + 1) * 128, :] = (1.0 / jnp.broadcast_to(total_row(b, 0), (128, 128))).T
+    leave(0)
+    leave(1)
+    final[2]()
+    leave(2)
+    pass_on(0)
+    final[3]()
+    leave(3)
+    pass_on(1)
+    pass_on(2)
+    pass_on(3)
     ol_ref[...] = jnp.log(total_row(0, 0)) - total_row(0, 4) * 10.0
-    og_ref[...] = partial_rows(0)
-    for b in (1, 3, 2):
-        arrived("out", b)
-    direction = og_ref[...] + ((rb[0].astype(F32) + rb[1].astype(F32)) + rb[2].astype(F32))
     scale = (jnp.broadcast_to(lmv[...], (128, 128)).T)[:, 0:1] * 10.0
+    projection = jnp.zeros((128, 1), F32)
+    for n in range(4):
+        cols = slice(n * 256, (n + 1) * 256)
+        for b in (1, 3):
+            for h in (0, 1):
+                arrived("out", b, n, h)
+        direction = partial_rows(0, cols) + (rb[0, n].astype(F32) + rb[1, n].astype(F32))
+        g = direction * scale
+        og_ref[:, cols] = g
+        projection = projection + jnp.sum(qin[:, cols].astype(F32) * g, axis=1, keepdims=True)
     xf = qin[...].astype(F32)
     q_scale = lax.rsqrt(jnp.sum(xf * xf, axis=1, keepdims=True) + EPS)
-    g = direction * scale
-    projection = jnp.sum(xf * g, axis=1, keepdims=True)
-    og_ref[...] = q_scale * g - (q_scale * q_scale * q_scale * projection) * xf
+    og_ref[...] = q_scale * og_ref[...] - (q_scale * q_scale * q_scale * projection) * xf
     for copy in copies.values():
         copy.wait_send()
 
@@ -352,8 +406,9 @@
             pltpu.VMEM((512, 128), F32),
             pltpu.VMEM((512, 128), F32),
             pltpu.VMEM((4, 8, 128), F32),
-            pltpu.VMEM((3, 128, 1024), BF16),
-            pltpu.VMEM((3, 128, 1024), BF16),
+            pltpu.VMEM((3, 4, 128, 256), BF16),
+            pltpu.VMEM((2, 4, 128, 256), BF16),
+            pltpu.VMEM((2, 4, 64, 256), BF16),
             pltpu.SemaphoreType.DMA((6,)),
             pltpu.SemaphoreType.DMA((count,)),
             pltpu.SemaphoreType.DMA((count,)),

time: 76.1 us -> 69.2 us (0.909); the launches traced: 76 us -> 68.2 us
  Pallas kernels: 72.9 us -> 65.1 us
    pallas_call x1, Pallas kernels: 72.9 us -> 65.1 us  [body(): pl.pallas_call(kernel, out_shape=(jax.ShapeDtypeStruct((128, 1024), F32),...]
where the time goes in v3:
time: 69.2 us; the launch traced here: 68.2 us
  Pallas kernels  65.1 us (94%)
  local copies, waits for them, and re-layouts  2.4 us (3%)
    pallas_call x1, Pallas kernels, body(): pl.pallas_call(kernel, out_shape=(jax.ShapeDtypeStruct((128, 1024), F32),...  65.1 us
    unnamed x4, local copies, waits for them, and re-layouts  2.4 us

profile of v3, /device:TPU:1, one launch (start us, length us, event | category | flops | bytes accessed | tf_op | source)
XLA Modules:
  0.0 68.2 jit_solution(17956713970469685047)
XLA Ops:
  0.6 65.1 %contrastive.1 = (f32[128,1024]{1,0:T(8,128)}, f32[1,128]{1,0:T(1,128)}) custom-call(bf16[128,1024]{1,0:T(8,128)(2,1)} %q_ref.1, bf16[64,1024]{1,0:T(8,128)(2,1)} %k_ref.1, s32[1,256]{1,0:T(1,128)} %pat_ref.1, s32[1,64]{1,0:T(1,128)} %bitcast.4, s32[1,128]{1,0:T(1,128)} %bitcast.5, f32[1,128]{1,0:T(1,128)} %bitcast.6), custom_call_target="tpu_custom_call" | custom-call | tf_op jit(solution)/shard_map/contrastive/pallas_call | solution.py:383
  65.7 0.0 copy-start
  65.8 1.9 %copy.10 = f32[128,1024]{1,0:T(8,128)} copy(f32[128,1024]{1,0:T(8,128)} %get-tuple-element.8) | data formatting | bytes 1048576
  67.6 0.0 copy-done
  67.6 0.5 copy.11
Async XLA Ops:
  65.7 1.9 %copy-start = (f32[1,128]{1,0:T(1,128)S(1)}, f32[1,128]{1,0:T(1,128)}, u32[]{:S(2)}) copy-start(f32[1,128]{1,0:T(1,128)} %get-tuple-element.5) | copy-start | bytes 1540

commit v4 on v3

--- a/solution.py
+++ b/solution.py
@@ -46,7 +46,9 @@
         for d in (1, 2, 3):
             ids("bx", k, d), ids("g", k, d)
     for k in range(8):
-        ids("sib", k)
+        if k != 4:
+            ids("sib", k)
+    ids("sw"), ids("sg", 0), ids("sg", 1), ids("sg", 2), ids("sg", 3)
     for n in range(4):
         for h in (0, 1):
             ids("rel", n, h), ids("out", 1, n, h), ids("out", 3, n, h)
@@ -54,7 +56,7 @@
 
 
 IDS = message_names()
-STAGES = (((0,),), ((1, 7),), ((2, 6),), ((3, 5),), ((4,),))
+STAGES = (((0,),), ((1, 7),), ((2, 6),), ((3, 5), (4,)))
 
 
 def kernel(q_ref, k_ref, pat_ref, cl_ref, pos_ref, lm_ref, og_ref, ol_ref, kin, qin, clv, lmv, kb, qb, mb, clx, clz,
@@ -164,8 +166,14 @@
         for d in (1, 3, 2):
             send(("bx", k, d), b_half(k, 0), b_half(k, d), at_x(d))
 
+    def to_sibling(j):
+        u, v = unit_of(4) * 4 + j, sibling_unit(4) * 4 + j
+        send(("sg", j), kb.at[u, 0], kb.at[v, 0], sibling)
+
     def half(k, j):
         arrived("g", k, j)
+        if k == 4:
+            to_sibling(j)
         if k < 3:
             send_g(k + 1, j, g_half(k, j))
         elif k > 4:
@@ -178,6 +186,11 @@
                     arrived("bx", k, d)
                 else:
                     arrived("xb", d)
+            if k == 4:
+                to_sibling(0)
+                u, v = unit_of(4) * 4, sibling_unit(4) * 4
+                send(("sw",), kb.at[u:u + 4, 1], kb.at[v:v + 4, 1], sibling)
+                continue
             send(("sib", k), kb.at[pl.ds(unit_of(k) * 4, 4)], kb.at[pl.ds(sibling_unit(k) * 4, 4)], sibling)
 
     def queries_on():
@@ -204,7 +217,11 @@
         arrived("q2", 3)
 
     def score(first, t, s, k):
-        if s == 1:
+        if s == 1 and k == 4:
+            arrived("sw")
+            for j in range(4):
+                arrived("sg", j)
+        elif s == 1:
             arrived("sib", k)
         unit = first + t
         keys = kb[unit * 4:unit * 4 + 4].reshape(256, 1024)
@@ -294,10 +311,11 @@
     run(wholes(4), scores(2))
     run(halves(4, (1,)), columns(2))
     share(3)
-    run(halves(4, (3, 2)), scores(3))
+    last = scores(3)
+    run(halves(4, (3,)), last[:2])
     share(4)
-    run(columns(3))
-    run(scores(4))
+    run(halves(4, (2,)), last[2:4])
+    run(last[4:])
 
     for b in range(4):
         rows = slice(b * 128, (b + 1) * 128)
@@ -341,7 +359,7 @@
         pb[1, n, lower] = (partial_rows(3, cols)[lower] + rl[1, n].astype(F32)).astype(BF16)
         send(("out", 3, n, 1), pb.at[1, n, lower], rb.at[1, n, lower], at_y(1))
 
-    final = columns(4)
+    final = columns(3)
     run(final[:2])
     for d in (1, 3, 2):
         arrived("tot", d)
@@ -397,8 +415,8 @@
             pltpu.VMEM((2, 8, 1, 256), I32),
             pltpu.VMEM((8, 256), F32),
             pltpu.VMEM((8, 256), F32),
-            pltpu.VMEM((512, 1024), BF16),
-            pltpu.VMEM((512, 1024), BF16),
+            pltpu.VMEM((512, 1536), BF16),
+            pltpu.VMEM((512, 1536), BF16),
             pltpu.VMEM((512, 256), F32),
             pltpu.VMEM((512, 1024), F32),
             pltpu.VMEM((512, 1024), F32),

time: 69.2 us -> 66.5 us (0.961)
  Pallas kernels: 65.1 us -> 62.3 us
    pallas_call x1, Pallas kernels: 65.1 us -> 62.3 us  [body(): pl.pallas_call(kernel, out_shape=(jax.ShapeDtypeStruct((128, 1024), F32),...]
where the time goes in v4:
time: 66.5 us; the launch traced here: 65.3 us
  Pallas kernels  62.3 us (94%)
  local copies, waits for them, and re-layouts  2.4 us (4%)
    pallas_call x1, Pallas kernels, body(): pl.pallas_call(kernel, out_shape=(jax.ShapeDtypeStruct((128, 1024), F32),...  62.3 us
    unnamed x4, local copies, waits for them, and re-layouts  2.4 us

profile of v4, /device:TPU:1, one launch (start us, length us, event | category | flops | bytes accessed | tf_op | source)
XLA Modules:
  0.0 65.3 jit_solution(12322705671027275110)
XLA Ops:
  0.6 62.3 %contrastive.1 = (f32[128,1024]{1,0:T(8,128)}, f32[1,128]{1,0:T(1,128)}) custom-call(bf16[128,1024]{1,0:T(8,128)(2,1)} %q_ref.1, bf16[64,1024]{1,0:T(8,128)(2,1)} %k_ref.1, s32[1,256]{1,0:T(1,128)} %pat_ref.1, s32[1,64]{1,0:T(1,128)} %bitcast.4, s32[1,128]{1,0:T(1,128)} %bitcast.5, f32[1,128]{1,0:T(1,128)} %bitcast.6), custom_call_target="tpu_custom_call" | custom-call | tf_op jit(solution)/shard_map/contrastive/pallas_call | solution.py:401
  62.9 0.0 copy-start
  62.9 1.9 %copy.10 = f32[128,1024]{1,0:T(8,128)} copy(f32[128,1024]{1,0:T(8,128)} %get-tuple-element.8) | data formatting | bytes 1048576
  64.8 0.0 copy-done
  64.8 0.5 copy.11
Async XLA Ops:
  62.9 1.9 %copy-start = (f32[1,128]{1,0:T(1,128)S(1)}, f32[1,128]{1,0:T(1,128)}, u32[]{:S(2)}) copy-start(f32[1,128]{1,0:T(1,128)} %get-tuple-element.5) | copy-start | bytes 1540

commit v5 on v4

--- a/solution.py
+++ b/solution.py
@@ -38,7 +38,7 @@
 def message_names():
     ids = Ids()
     for d in (1, 2, 3):
-        ids("xa", d), ids("xb", d), ids("cx", d), ids("meta", d), ids("tot", d)
+        ids("xa", d), ids("xb", d), ids("cx", d), ids("meta", d), ids("tot", d), ids("ps", d)
     for name in (("q", 1), ("q", 3), ("q2", 1), ("q2", 3), ("cs",)):
         ids(*name)
     for k in range(1, 8):
@@ -238,17 +238,20 @@
                                    preferred_element_type=F32)
         for b in range(4):
             rows = slice(b * 128, (b + 1) * 128)
+            sums, picked = [], []
             for h in range(2):
                 cols = slice(h * 128, (h + 1) * 128)
                 st = sbuf[rows, cols]
                 is_pos = pos_t[rows, :] == key_id[:, cols]
                 one = jnp.where(is_pos, 1.0, 0.0)
                 w = jnp.exp2(st * EXP2_SCALE) * jnp.maximum(one, amb[b:b + 1, cols])
-                tot[rows, :] += w
-                pss[rows, :] += st * one
+                sums.append(w)
+                picked.append(st * one)
                 to = slice(t * 256 + h * 128, t * 256 + h * 128 + 128)
                 wbuf[rows, to] = w.astype(BF16)
                 obuf[rows, to] = one.astype(BF16)
+            tot[rows, :] += sums[0] + sums[1]
+            pss[rows, :] += picked[0] + picked[1]
 
     def column(first, units, n):
         cols = slice(n * 256, (n + 1) * 256)
@@ -308,9 +311,9 @@
     share(1)
     run(events(3), scores(1) + columns(1))
     share(2)
-    run(wholes(4), scores(2))
-    run(halves(4, (1,)), columns(2))
+    run(wholes(4) + halves(4, (1,)), scores(2))
     share(3)
+    run(columns(2))
     last = scores(3)
     run(halves(4, (3,)), last[:2])
     share(4)
@@ -319,16 +322,20 @@
 
     for b in range(4):
         rows = slice(b * 128, (b + 1) * 128)
-        tb[0, b:b + 1, :] = jnp.sum(tot[rows, :].T, axis=0, keepdims=True)
-        tb[0, 4 + b:5 + b, :] = jnp.sum(pss[rows, :].T, axis=0, keepdims=True)
+        tb[0, 0, b:b + 1, :] = jnp.sum(tot[rows, :].T, axis=0, keepdims=True)
     for d in (2, 1, 3):
-        send(("tot", d), tb.at[0], tb.at[d], at_y(d))
+        send(("tot", d), tb.at[0, 0], tb.at[d, 0], at_y(d))
+    for b in range(4):
+        rows = slice(b * 128, (b + 1) * 128)
+        tb[0, 1, b:b + 1, :] = jnp.sum(pss[rows, :].T, axis=0, keepdims=True)
+    for d in (2, 1, 3):
+        send(("ps", d), tb.at[0, 1], tb.at[d, 1], at_y(d))
 
     def total_row(b, base):
-        row = tb[0, base + b:base + b + 1, :]
+        row = tb[0, base, b:b + 1, :]
         for d in (1, 2, 3):
-            i = base + (b - d) % 4
-            row = row + tb[d, i:i + 1, :]
+            i = (b - d) % 4
+            row = row + tb[d, base, i:i + 1, :]
         return row
 
     def partial_rows(b, cols):
@@ -369,13 +376,15 @@
     leave(1)
     final[2]()
     leave(2)
-    pass_on(0)
     final[3]()
     leave(3)
+    pass_on(0)
     pass_on(1)
     pass_on(2)
     pass_on(3)
-    ol_ref[...] = jnp.log(total_row(0, 0)) - total_row(0, 4) * 10.0
+    for d in (1, 3, 2):
+        arrived("ps", d)
+    ol_ref[...] = jnp.log(total_row(0, 0)) - total_row(0, 1) * 10.0
     scale = (jnp.broadcast_to(lmv[...], (128, 128)).T)[:, 0:1] * 10.0
     projection = jnp.zeros((128, 1), F32)
     for n in range(4):
@@ -423,7 +432,7 @@
             pltpu.VMEM((512, 128), F32),
             pltpu.VMEM((512, 128), F32),
             pltpu.VMEM((512, 128), F32),
-            pltpu.VMEM((4, 8, 128), F32),
+            pltpu.VMEM((4, 2, 8, 128), F32),
             pltpu.VMEM((3, 4, 128, 256), BF16),
             pltpu.VMEM((2, 4, 128, 256), BF16),
             pltpu.VMEM((2, 4, 64, 256), BF16),

time: 66.5 us -> 65.5 us (0.985); the launches traced: 65.3 us -> 65.4 us
  no operation moved by 1% of the time
where the time goes in v5:
time: 65.5 us; the launch traced here: 65.4 us
  Pallas kernels  62.3 us (95%)
  local copies, waits for them, and re-layouts  2.4 us (4%)
    pallas_call x1, Pallas kernels, body(): pl.pallas_call(kernel, out_shape=(jax.ShapeDtypeStruct((128, 1024), F32),...  62.3 us
    unnamed x4, local copies, waits for them, and re-layouts  2.4 us

profile of v5, /device:TPU:1, one launch (start us, length us, event | category | flops | bytes accessed | tf_op | source)
XLA Modules:
  0.0 65.4 jit_solution(5931980365443527345)
XLA Ops:
  0.6 62.3 %contrastive.1 = (f32[128,1024]{1,0:T(8,128)}, f32[1,128]{1,0:T(1,128)}) custom-call(bf16[128,1024]{1,0:T(8,128)(2,1)} %q_ref.1, bf16[64,1024]{1,0:T(8,128)(2,1)} %k_ref.1, s32[1,256]{1,0:T(1,128)} %pat_ref.1, s32[1,64]{1,0:T(1,128)} %bitcast.4, s32[1,128]{1,0:T(1,128)} %bitcast.5, f32[1,128]{1,0:T(1,128)} %bitcast.6), custom_call_target="tpu_custom_call" | custom-call | tf_op jit(solution)/shard_map/contrastive/pallas_call | solution.py:410
  62.9 0.0 copy-start
  63.0 1.9 %copy.10 = f32[128,1024]{1,0:T(8,128)} copy(f32[128,1024]{1,0:T(8,128)} %get-tuple-element.8) | data formatting | bytes 1048576
  64.8 0.0 copy-done
  64.8 0.5 copy.11
Async XLA Ops:
  62.9 1.9 %copy-start = (f32[1,128]{1,0:T(1,128)S(1)}, f32[1,128]{1,0:T(1,128)}, u32[]{:S(2)}) copy-start(f32[1,128]{1,0:T(1,128)} %get-tuple-element.5) | copy-start | bytes 1540

commit v6 on v5

--- a/solution.py
+++ b/solution.py
@@ -309,8 +309,9 @@
     prepare()
     run(events(2), scores(0) + columns(0))
     share(1)
-    run(events(3), scores(1) + columns(1))
+    run(events(3), scores(1) + columns(1)[:2])
     share(2)
+    run(columns(1)[2:])
     run(wholes(4) + halves(4, (1,)), scores(2))
     share(3)
     run(columns(2))
@@ -367,17 +368,21 @@
         send(("out", 3, n, 1), pb.at[1, n, lower], rb.at[1, n, lower], at_y(1))
 
     final = columns(3)
-    run(final[:2])
+    run(final[:3])
     for d in (1, 3, 2):
         arrived("tot", d)
     for b in (2, 1, 3, 0):
         tot[b * 128:(b + 1) * 128, :] = (1.0 / jnp.broadcast_to(total_row(b, 0), (128, 128))).T
     leave(0)
     leave(1)
-    final[2]()
     leave(2)
     final[3]()
     leave(3)
+    for n in range(4):
+        og_ref[:, n * 256:(n + 1) * 256] = partial_rows(0, slice(n * 256, (n + 1) * 256))
+    own = qin[...].astype(F32)
+    q_scale = lax.rsqrt(jnp.sum(own * own, axis=1, keepdims=True) + EPS)
+    scale = (jnp.broadcast_to(lmv[...], (128, 128)).T)[:, 0:1] * 10.0
     pass_on(0)
     pass_on(1)
     pass_on(2)
@@ -385,19 +390,17 @@
     for d in (1, 3, 2):
         arrived("ps", d)
     ol_ref[...] = jnp.log(total_row(0, 0)) - total_row(0, 1) * 10.0
-    scale = (jnp.broadcast_to(lmv[...], (128, 128)).T)[:, 0:1] * 10.0
     projection = jnp.zeros((128, 1), F32)
     for n in range(4):
         cols = slice(n * 256, (n + 1) * 256)
         for b in (1, 3):
             for h in (0, 1):
                 arrived("out", b, n, h)
-        direction = partial_rows(0, cols) + (rb[0, n].astype(F32) + rb[1, n].astype(F32))
+        direction = og_ref[:, cols] + (rb[0, n].astype(F32) + rb[1, n].astype(F32))
         g = direction * scale
         og_ref[:, cols] = g
         projection = projection + jnp.sum(qin[:, cols].astype(F32) * g, axis=1, keepdims=True)
     xf = qin[...].astype(F32)
-    q_scale = lax.rsqrt(jnp.sum(xf * xf, axis=1, keepdims=True) + EPS)
     og_ref[...] = q_scale * og_ref[...] - (q_scale * q_scale * q_scale * projection) * xf
     for copy in copies.values():
         copy.wait_send()

time: 65.5 us -> 65.6 us (level)
  no operation moved by 1% of the time
where the time goes in v6:
time: 65.6 us; the launch traced here: 65.1 us
  Pallas kernels  62.1 us (95%)
  local copies, waits for them, and re-layouts  2.4 us (4%)
    pallas_call x1, Pallas kernels, body(): pl.pallas_call(kernel, out_shape=(jax.ShapeDtypeStruct((128, 1024), F32),...  62.1 us
    unnamed x4, local copies, waits for them, and re-layouts  2.4 us

profile of v6, /device:TPU:1, one launch (start us, length us, event | category | flops | bytes accessed | tf_op | source)
XLA Modules:
  0.0 65.1 jit_solution(12972745478221237910)
XLA Ops:
  0.6 62.1 %contrastive.1 = (f32[128,1024]{1,0:T(8,128)}, f32[1,128]{1,0:T(1,128)}) custom-call(bf16[128,1024]{1,0:T(8,128)(2,1)} %q_ref.1, bf16[64,1024]{1,0:T(8,128)(2,1)} %k_ref.1, s32[1,256]{1,0:T(1,128)} %pat_ref.1, s32[1,64]{1,0:T(1,128)} %bitcast.4, s32[1,128]{1,0:T(1,128)} %bitcast.5, f32[1,128]{1,0:T(1,128)} %bitcast.6), custom_call_target="tpu_custom_call" | custom-call | tf_op jit(solution)/shard_map/contrastive/pallas_call | solution.py:413
  62.7 0.0 copy-start
  62.7 1.9 %copy.10 = f32[128,1024]{1,0:T(8,128)} copy(f32[128,1024]{1,0:T(8,128)} %get-tuple-element.8) | data formatting | bytes 1048576
  64.6 0.0 copy-done
  64.6 0.5 copy.11
Async XLA Ops:
  62.7 1.9 %copy-start = (f32[1,128]{1,0:T(1,128)S(1)}, f32[1,128]{1,0:T(1,128)}, u32[]{:S(2)}) copy-start(f32[1,128]{1,0:T(1,128)} %get-tuple-element.5) | copy-start | bytes 1540
